TPU v7x, 256 devices: a whole 4x4x8 slice. The times are simulated.
256 devices in a mesh: grp: 16 (over z, core), pool: 16 (over y, x).
Axes of the slice: x: 4, y: 4, z: 8, core: 2. Of those that a mesh axis runs over, the one named last changes fastest.
Arguments:
- tokens: bfloat16 [16, 2048, 2048], P('grp', 'pool'), may hold values from -6 to 6
- ln_gain: bfloat16 [2048], replicated, may hold values from 0.099609375 to 1.8984375
- w_qkv: bfloat16 [2048, 16, 192], P('grp', 'pool'), may hold values from -0.25 to 0.25
- w_out: bfloat16 [16, 64, 2048], P('pool', None, 'grp'), may hold values from -0.1875 to 0.1875
- w_fc: bfloat16 [2048, 8192], P(None, 'pool'), may hold values from -0.125 to 0.125
- w_proj: bfloat16 [8192, 2048], P('pool'), may hold values from -0.0625 to 0.0625
- pool_kv: bfloat16 [16, 256, 16, 16, 128], P('grp', 'pool'), may hold values from -160 to 160, as said below
- block_table: int32 [16, 8, 128], P('grp'), may hold values from 0 to 255, as said below
- block_count: int32 [16, 8], P('grp'), may hold values from 1 to 128, as said below
- lengths: int32 [16, 8], P('grp'), may hold values from 1 to 512, 2048 in all within a row
Outputs:
- layer_out: bfloat16 [16, 2048, 2048], P('grp', 'pool')
Inputs may be any that keep to these rules, and one draw needn't show every extreme that they name: `block_table`: the first block_count entries of a request's row are distinct; later entries are valid block numbers and are not used. `block_count`: in every group some request uses 128 blocks. `pool_kv`: in the last dimension the first 64 entries are a head's key, already rotated, and the last 64 its value.
All inputs are finite; a program needn't handle non-finite values.
Results may differ from a plain program's by a relative error of at most 0.017.
Values may be sent and summed in bfloat16 or wider, within the bound.
No kernel may reach another device: no remote copies, remote signals or barrier semaphores. Data moves between devices by JAX's collectives and lax.ppermute only.
A program may use at most 128 MiB of HBM per device.

v0:
```python
import jax
import jax.numpy as jnp
from jax import lax
from jax.sharding import PartitionSpec as P

ROT = 32


epsilon = 1e-05


def layer_norm(rows, gain):
    values = rows.astype(jnp.float32)
    centred = values - jnp.mean(values, axis=-1, keepdims=True)
    variance = jnp.mean(centred * centred, axis=-1, keepdims=True)
    return (centred * lax.rsqrt(variance + epsilon) * gain.astype(jnp.float32)).astype(jnp.bfloat16)


def rotate(field, where):
    half = ROT // 2
    frequency = 10000.0 ** (-2.0 * jnp.arange(half, dtype=jnp.float32) / ROT)
    angle = where.astype(jnp.float32)[:, None] * frequency[None, :]
    cosine = jnp.cos(angle)[:, None, :]
    sine = jnp.sin(angle)[:, None, :]
    first = field[..., :half]
    second = field[..., half:ROT]
    return jnp.concatenate(
        [first * cosine - second * sine, second * cosine + first * sine, field[..., ROT:]], axis=-1
    )


def request_info(request_lengths, counts, table, group_tok, pool_blocks, block_len):
    ends = jnp.cumsum(request_lengths)
    starts = ends - request_lengths
    token_index = jnp.arange(group_tok, dtype=jnp.int32)
    inside = (token_index[:, None] >= starts[None, :]) & (token_index[:, None] < ends[None, :])
    numbers = jnp.arange(request_lengths.shape[0], dtype=jnp.int32)
    request_of = jnp.sum(jnp.where(inside, numbers[None, :], 0), axis=-1)
    position = (
        jnp.sum(jnp.where(inside, (counts * block_len - starts)[None, :], 0), axis=-1) + token_index
    )
    listed = jnp.arange(table.shape[1], dtype=jnp.int32)[None, :] < counts[:, None]
    member = jnp.any(
        (table[:, :, None] == jnp.arange(pool_blocks, dtype=jnp.int32)[None, None, :])
        & listed[:, :, None],
        axis=1,
    )
    allowed = (
        jnp.dot(
            inside.astype(jnp.float32),
            member.astype(jnp.float32),
            preferred_element_type=jnp.float32,
        )
        > 0.5
    )
    return (request_of, position, allowed)


def partial_attention(queries, keys, values, visible):
    scale = queries.shape[-1] ** (-0.5)
    scores = jnp.einsum("rhe,khe->rhk", queries, keys, preferred_element_type=jnp.float32) * scale
    scores = jnp.where(visible[:, None, :], scores, -1e30)
    highest = jnp.max(scores, axis=-1)
    weights = jnp.where(visible[:, None, :], jnp.exp(scores - highest[..., None]), 0.0).astype(
        jnp.bfloat16
    )
    total = jnp.sum(weights.astype(jnp.float32), axis=-1)
    summed = jnp.einsum("rhk,khe->rhe", weights, values, preferred_element_type=jnp.float32)
    return (highest, total, summed)


def combine(highs, totals, sums, high_new, total_new, sum_new):
    largest = jnp.maximum(jnp.max(highs, axis=0), high_new)
    factor = jnp.exp(highs - largest[None])
    factor_new = jnp.exp(high_new - largest)
    total = jnp.sum(factor * totals, axis=0) + factor_new * total_new
    summed = jnp.sum(factor[..., None] * sums, axis=0) + factor_new[..., None] * sum_new
    return summed / total[..., None]


def per_device(
    tokens, ln_gain, w_qkv, w_out, w_fc, w_proj, pool_kv, block_table, block_count, lengths
):
    holders = lax.axis_size("pool")
    rows_dev = tokens.shape[1]
    group_tok = rows_dev * holders
    local_pool = pool_kv[0]
    blk_dev, block_len, heads_all, paired = local_pool.shape
    head_dim = paired // 2
    pool_blocks = blk_dev * holders
    qkv_weight, out_weight = (
        lax.all_gather(w_qkv, "grp", axis=0, tiled=True),
        lax.all_gather(w_out, "grp", axis=2, tiled=True),
    )
    heads_dev = qkv_weight.shape[1]
    request_of, position, allowed = request_info(
        lengths[0], block_count[0], block_table[0], group_tok, pool_blocks, block_len
    )
    normed = layer_norm(tokens[0], ln_gain)
    units = w_fc.shape[1]
    piece = lax.all_gather(normed, "pool", axis=0, tiled=True)
    count = piece.shape[0]
    hidden_rows = jax.nn.gelu(
        jnp.dot(piece, w_fc, preferred_element_type=jnp.float32), approximate=True
    ).astype(jnp.bfloat16)
    projected = jnp.einsum("td,dhe->the", piece, qkv_weight, preferred_element_type=jnp.float32)
    query_rows = rotate(projected[..., :head_dim], position)
    key_rows = rotate(projected[..., head_dim : 2 * head_dim], position)
    joined = jnp.concatenate(
        [query_rows, key_rows, projected[..., 2 * head_dim :]], axis=-1
    ).astype(jnp.bfloat16)
    results = jnp.concatenate(
        [hidden_rows, joined.reshape(count, heads_dev * 3 * head_dim)], axis=1
    )
    hidden = results[:, :units]
    joined = results[:, units:].reshape(group_tok, heads_dev, 3 * head_dim)
    query = joined[..., :head_dim]
    key_new = joined[..., head_dim : 2 * head_dim]
    value_new = joined[..., 2 * head_dim :]
    block_rows = min(512, group_tok)
    block_total = group_tok // block_rows
    block_ids = jnp.arange(block_total, dtype=jnp.int32)
    token_index = jnp.arange(group_tok, dtype=jnp.int32)

    def new_block(block_index):
        begin = block_index * block_rows
        query_rows = lax.dynamic_slice_in_dim(query, begin, block_rows)
        owners = lax.dynamic_slice_in_dim(request_of, begin, block_rows)
        places = lax.dynamic_slice_in_dim(token_index, begin, block_rows)
        visible = (owners[:, None] == request_of[None, :]) & (
            token_index[None, :] <= places[:, None]
        )
        return partial_attention(query_rows, key_new, value_new, visible)

    high_new, total_new, sum_new = lax.map(new_block, block_ids)
    high_new = high_new.reshape(group_tok, heads_dev)
    total_new = total_new.reshape(group_tok, heads_dev)
    sum_new = sum_new.reshape(group_tok, heads_dev, head_dim)
    pooled = lax.all_to_all(local_pool, "pool", split_axis=2, concat_axis=0, tiled=True)
    keys_pool = pooled[..., :head_dim].reshape(pool_blocks * block_len, heads_dev, head_dim)
    values_pool = pooled[..., head_dim:].reshape(pool_blocks * block_len, heads_dev, head_dim)

    def pool_block(block_index):
        begin = block_index * block_rows
        query_rows = lax.dynamic_slice_in_dim(query, begin, block_rows)
        visible = jnp.repeat(
            lax.dynamic_slice_in_dim(allowed, begin, block_rows), block_len, axis=1
        )
        return partial_attention(query_rows, keys_pool, values_pool, visible)

    highs, totals, sums = lax.map(pool_block, block_ids)
    highs = highs.reshape(1, group_tok, heads_dev)
    totals = totals.reshape(1, group_tok, heads_dev)
    sums = sums.reshape(1, group_tok, heads_dev, head_dim)
    attention = combine(highs, totals, sums, high_new, total_new, sum_new).astype(jnp.bfloat16)
    attention = attention.reshape(group_tok, heads_dev * head_dim)
    out_rows = out_weight.reshape(heads_dev * head_dim, out_weight.shape[2])
    summed = lax.psum_scatter(
        (
            jnp.dot(attention, out_rows, preferred_element_type=jnp.float32)
            + jnp.dot(hidden, w_proj, preferred_element_type=jnp.float32)
        ).astype(jnp.bfloat16),
        "pool",
        scatter_dimension=0,
        tiled=True,
    ).astype(jnp.float32)
    return (tokens[0].astype(jnp.float32) + summed).astype(jnp.bfloat16)[None]


def solution(mesh):
    in_specs = (
        P("grp", "pool", None),
        P(),
        P("grp", "pool", None),
        P("pool", None, "grp"),
        P(None, "pool"),
        P("pool", None),
        P("grp", "pool", None, None, None),
        P("grp", None, None),
        P("grp", None),
        P("grp", None),
    )
    out_specs = P("grp", "pool", None)
    return jax.shard_map(
        per_device, mesh=mesh, in_specs=in_specs, out_specs=out_specs, check_vma=False
    )
```

profile of v0, /device:TPU:160, one launch (start us, length us, event | category | flops | bytes accessed | tf_op | source)
XLA Modules:
  0.0 357.8 jit_solution(7055959415550061387)
XLA Ops:
  10.0 2.2 fusion.44
  12.2 2.5 copy.39
  14.7 7.0 %all-to-all-start = ((bf16[16,16,16,128]{3,1,0,2:T(8,128)(2,1)}), bf16[16,16,16,128]{3,1,0,2:T(8,128)(2,1)S(1)}, u32[]{:S(2)}, u32[]{:S(2)}) async-start(bf16[16,16,16,128]{3,1,0,2:T(8,128)(2,1)} %bitcast.193), calls=%async_computation | async-start | bytes 2097152 | tf_op jit(solution)/shard_map/all_to_all | solution.py:139
  22.1 17.2 %all_gather.11 = bf16[1,64,2048]{2,1,0:T(8,128)(2,1)} all-gather(bf16[1,64,128]{2,1,0:T(8,128)(2,1)S(1)} %copy-done.5), channel_id=1, replica_groups=mesh['grp'=16,'pool'=16] {'grp'}, dimensions={2}, use_global_device_ids=true | all-gather | bytes 278528 | tf_op jit(solution)/shard_map/all_gather | solution.py:93
  41.7 18.7 %all_gather.10 = bf16[2048,1,192]{0,2,1:T(8,128)(2,1)} all-gather(bf16[128,1,192]{0,2,1:T(8,128)(2,1)S(1)} %copy-done.4), channel_id=1, replica_groups=mesh['grp'=16,'pool'=16] {'grp'}, dimensions={0}, use_global_device_ids=true | all-gather | bytes 835584 | tf_op jit(solution)/shard_map/all_gather | solution.py:92
  60.4 1.8 fusion.83
  62.2 1.5 copy.28
  63.8 1.5 copy.27
  65.3 29.9 %all-gather.2.cloned.1.call-done = bf16[2048,2048]{1,0:T(8,128)(2,1)} async-done(((bf16[128,2048]{1,0:T(8,128)(2,1)}), bf16[2048,2048]{1,0:T(8,128)(2,1)}) %all-gather.2.cloned.1.call-update) | async-done | bytes 8388624 | tf_op jit(solution)/shard_map/all_gather | solution.py:101
  95.2 6.4 %fusion.84 = (bf16[2048,1,192]{0,2,1:T(8,128)(2,1)S(1)}, f32[2048,1,192]{0,2,1:T(8,128)S(1)}) fusion(bf16[2048,2048]{1,0:T(8,128)(2,1)} %all-gather.2.cloned.1.call-done, bf16[2048,1,192]{0,2,1:T(8,128)(2,1)} %all_gather.10), kind=kOutput, calls=%fused_computation.116 | convolution fusion | flops 1611005952 | bytes 11534336 | tf_op jit(solution)/shard_map/td,dhe->the/dot_general | solution.py:106
  105.8 44.9 %while.30 = (s32[]{:T(128)}, f32[4,512,1]{1,2,0:T(1,128)}, f32[4,512,1]{1,2,0:T(1,128)}, f32[4,512,1,64]{1,0,3,2:T(4,128)}, s32[4]{0:T(128)}, /*index=5*/s32[204...) while((s32[]{:T(128)}, f32[4,512,1]{1,2,0:T(1,128)}, ...), condition=%wide.region_13.14_spmd.clone, body=%wide.region_10.13_spmd.clone.sunk | while | flops 285211648 | bytes 13891803 | solution.py:135
  107.8 2.3 fusion.106
  110.1 1.8 convert_reduce_fusion.6
  113.4 3.6 %dynamic_update_slice.34 = f32[4,512,1,64]{1,0,3,2:T(4,128)} dynamic-update-slice(f32[4,512,1,64]{1,0,3,2:T(4,128)} %get-tuple-element.402, f32[1,512,1,64]{1,0,3,2:T(1,128)S(1)} %copy.47, s32[]{:T(128)S(6)} %copy.58, s32[]{:T(128)} %constant.48.clone.1..sunk.1, s32[]{:T(128)} %constant.48.clone.1..sunk.1, s32[]{:T(128)} %constant.48.clone.1..sunk.1) | dynamic-update-slice | bytes 262148 | tf_op jit(solution)/shard_map/while/body/jit(dynamic_update_index_in_dim)/dynamic_update_slice | solution.py:135
  119.0 2.3 fusion.106
  121.3 1.8 convert_reduce_fusion.6
  124.6 3.6 %dynamic_update_slice.34 = f32[4,512,1,64]{1,0,3,2:T(4,128)} dynamic-update-slice(f32[4,512,1,64]{1,0,3,2:T(4,128)} %get-tuple-element.402, f32[1,512,1,64]{1,0,3,2:T(1,128)S(1)} %copy.47, s32[]{:T(128)S(6)} %copy.58, s32[]{:T(128)} %constant.48.clone.1..sunk.1, s32[]{:T(128)} %constant.48.clone.1..sunk.1, s32[]{:T(128)} %constant.48.clone.1..sunk.1) | dynamic-update-slice | bytes 262148 | tf_op jit(solution)/shard_map/while/body/jit(dynamic_update_index_in_dim)/dynamic_update_slice | solution.py:135
  130.3 2.3 fusion.106
  132.6 1.8 convert_reduce_fusion.6
  135.9 3.6 %dynamic_update_slice.34 = f32[4,512,1,64]{1,0,3,2:T(4,128)} dynamic-update-slice(f32[4,512,1,64]{1,0,3,2:T(4,128)} %get-tuple-element.402, f32[1,512,1,64]{1,0,3,2:T(1,128)S(1)} %copy.47, s32[]{:T(128)S(6)} %copy.58, s32[]{:T(128)} %constant.48.clone.1..sunk.1, s32[]{:T(128)} %constant.48.clone.1..sunk.1, s32[]{:T(128)} %constant.48.clone.1..sunk.1) | dynamic-update-slice | bytes 262148 | tf_op jit(solution)/shard_map/while/body/jit(dynamic_update_index_in_dim)/dynamic_update_slice | solution.py:135
  141.5 2.3 fusion.106
  143.8 1.8 convert_reduce_fusion.6
  147.1 3.6 %dynamic_update_slice.34 = f32[4,512,1,64]{1,0,3,2:T(4,128)} dynamic-update-slice(f32[4,512,1,64]{1,0,3,2:T(4,128)} %get-tuple-element.402, f32[1,512,1,64]{1,0,3,2:T(1,128)S(1)} %copy.47, s32[]{:T(128)S(6)} %copy.58, s32[]{:T(128)} %constant.48.clone.1..sunk.1, s32[]{:T(128)} %constant.48.clone.1..sunk.1, s32[]{:T(128)} %constant.48.clone.1..sunk.1) | dynamic-update-slice | bytes 262148 | tf_op jit(solution)/shard_map/while/body/jit(dynamic_update_index_in_dim)/dynamic_update_slice | solution.py:135
  150.8 2.2 reshape.624
  153.9 75.7 %while.29 = (s32[]{:T(128)}, f32[4,512,1]{1,2,0:T(1,128)S(1)}, f32[4,512,1]{1,2,0:T(1,128)S(1)}, f32[4,512,1,64]{1,0,3,2:T(4,128)}, s32[4]{0:T(128)S(1)}, /*inde...) while((s32[]{:T(128)}, f32[4,512,1]{1,2,0:T(1,128)S(1)}, ...), condition=%wide.region_8.9_spmd, body=%wide.region_5.8_spmd.sunk | while | flops 557841408 | bytes 38090956 | solution.py:151
  157.0 4.5 %copy.45 = pred[512,1,4096]{2,0,1:T(32,128)(4,1)S(1)} copy(pred[512,1,4096]{0,2,1:T(8,128)(4,1)S(1)} %bitcast.191) | data formatting | bytes 4194304 | tf_op jit(solution)/shard_map/while/body/eval_jaxpr/broadcast_in_dim;while/body/eval_jaxpr/reshape | solution.py:62
  161.5 2.8 fusion.102
  164.3 3.3 convert_reduce_fusion.5
  167.6 1.4 fusion.103
  169.2 3.6 %dynamic_update_slice.32 = f32[4,512,1,64]{1,0,3,2:T(4,128)} dynamic-update-slice(f32[4,512,1,64]{1,0,3,2:T(4,128)} %get-tuple-element.443, f32[1,512,1,64]{1,0,3,2:T(1,128)S(1)} %copy.46, s32[]{:T(128)S(6)} %copy.70, s32[]{:T(128)} %constant.48.clone.1..sunk, s32[]{:T(128)} %constant.48.clone.1..sunk, s32[]{:T(128)} %constant.48.clone.1..sunk) | dynamic-update-slice | bytes 262148 | tf_op jit(solution)/shard_map/while/body/jit(dynamic_update_index_in_dim)/dynamic_update_slice | solution.py:135
  175.9 4.5 %copy.45 = pred[512,1,4096]{2,0,1:T(32,128)(4,1)S(1)} copy(pred[512,1,4096]{0,2,1:T(8,128)(4,1)S(1)} %bitcast.191) | data formatting | bytes 4194304 | tf_op jit(solution)/shard_map/while/body/eval_jaxpr/broadcast_in_dim;while/body/eval_jaxpr/reshape | solution.py:62
  180.4 2.8 fusion.102
  183.2 3.3 convert_reduce_fusion.5
  186.5 1.4 fusion.103
  188.1 3.6 %dynamic_update_slice.32 = f32[4,512,1,64]{1,0,3,2:T(4,128)} dynamic-update-slice(f32[4,512,1,64]{1,0,3,2:T(4,128)} %get-tuple-element.443, f32[1,512,1,64]{1,0,3,2:T(1,128)S(1)} %copy.46, s32[]{:T(128)S(6)} %copy.70, s32[]{:T(128)} %constant.48.clone.1..sunk, s32[]{:T(128)} %constant.48.clone.1..sunk, s32[]{:T(128)} %constant.48.clone.1..sunk) | dynamic-update-slice | bytes 262148 | tf_op jit(solution)/shard_map/while/body/jit(dynamic_update_index_in_dim)/dynamic_update_slice | solution.py:135
  194.8 4.5 %copy.45 = pred[512,1,4096]{2,0,1:T(32,128)(4,1)S(1)} copy(pred[512,1,4096]{0,2,1:T(8,128)(4,1)S(1)} %bitcast.191) | data formatting | bytes 4194304 | tf_op jit(solution)/shard_map/while/body/eval_jaxpr/broadcast_in_dim;while/body/eval_jaxpr/reshape | solution.py:62
  199.3 2.8 fusion.102
  202.1 3.3 convert_reduce_fusion.5
  205.5 1.4 fusion.103
  207.0 3.6 %dynamic_update_slice.32 = f32[4,512,1,64]{1,0,3,2:T(4,128)} dynamic-update-slice(f32[4,512,1,64]{1,0,3,2:T(4,128)} %get-tuple-element.443, f32[1,512,1,64]{1,0,3,2:T(1,128)S(1)} %copy.46, s32[]{:T(128)S(6)} %copy.70, s32[]{:T(128)} %constant.48.clone.1..sunk, s32[]{:T(128)} %constant.48.clone.1..sunk, s32[]{:T(128)} %constant.48.clone.1..sunk) | dynamic-update-slice | bytes 262148 | tf_op jit(solution)/shard_map/while/body/jit(dynamic_update_index_in_dim)/dynamic_update_slice | solution.py:135
  213.7 4.5 %copy.45 = pred[512,1,4096]{2,0,1:T(32,128)(4,1)S(1)} copy(pred[512,1,4096]{0,2,1:T(8,128)(4,1)S(1)} %bitcast.191) | data formatting | bytes 4194304 | tf_op jit(solution)/shard_map/while/body/eval_jaxpr/broadcast_in_dim;while/body/eval_jaxpr/reshape | solution.py:62
  218.2 2.8 fusion.102
  221.0 3.3 convert_reduce_fusion.5
  225.9 3.6 %dynamic_update_slice.32 = f32[4,512,1,64]{1,0,3,2:T(4,128)} dynamic-update-slice(f32[4,512,1,64]{1,0,3,2:T(4,128)} %get-tuple-element.443, f32[1,512,1,64]{1,0,3,2:T(1,128)S(1)} %copy.46, s32[]{:T(128)S(6)} %copy.70, s32[]{:T(128)} %constant.48.clone.1..sunk, s32[]{:T(128)} %constant.48.clone.1..sunk, s32[]{:T(128)} %constant.48.clone.1..sunk) | dynamic-update-slice | bytes 262148 | tf_op jit(solution)/shard_map/while/body/jit(dynamic_update_index_in_dim)/dynamic_update_slice | solution.py:135
  231.7 15.9 %fusion.32 = f32[2048,2048]{1,0:T(8,128)} fusion(bf16[512,2048]{1,0:T(8,128)(2,1)S(1)} %copy-done, bf16[2048,2048]{1,0:T(8,128)(2,1)} %all-gather.2.cloned.1.call-done, bf16[2048,512]{1,0:T(8,128)(2,1)} %param.18), kind=kOutput, calls=%fused_computation.44 | convolution fusion | flops 8599371776 | bytes 29360128 | tf_op jit(solution)/shard_map/dot_general | solution.py:161
  247.6 11.4 %add_convert_fusion = bf16[2048,2048]{1,0:T(8,128)(2,1)} fusion(f32[2048,2048]{1,0:T(8,128)} %fusion.32, bf16[1,64,2048]{2,1,0:T(8,128)(2,1)S(1)} %copy-done.3, f32[2048,1,1,1,1,1,64]{0,6,5,4,3,2,1:T(8,128)S(1)} %copy-done.2, f32[2048,1,1,1,1,1,64]{0,6,5,4,3,2,1:T(8,128)S(1)} %reshape.623, f32[2048]{0:T(1024)S(1)} %get-tuple-element.222, ...), kind=kOutput, calls=%fused_computation.32 | convolution fusion | flops 545914880 | bytes 26501120 | tf_op jit(solution)/shard_map/dot_general | solution.py:160
  259.0 89.9 %reduce-scatter.2.cloned.1.call-done = bf16[128,2048]{1,0:T(8,128)(2,1)} async-done(((bf16[2048,2048]{1,0:T(8,128)(2,1)}), bf16[128,2048]{1,0:T(8,128)(2,1)}) %reduce-scatter.2.cloned.1.call-update) | async-done | bytes 524304 | tf_op jit(solution)/shard_map/reduce_scatter | solution.py:158
  348.9 2.0 fusion.49
  (103 shorter events, 36.2 us)
Async XLA Ops:
  6.5 225.2 %copy-start = (bf16[512,2048]{1,0:T(8,128)(2,1)S(1)}, bf16[512,2048]{1,0:T(8,128)(2,1)}, u32[]{:S(2)}) copy-start(bf16[512,2048]{1,0:T(8,128)(2,1)} %param.19) | copy-start | bytes 6291460
  6.5 15.2 %copy-start.7 = (s32[1,8]{1,0:T(1,128)S(1)}, s32[1,8]{1,0:T(1,128)}, u32[]{:S(2)}) copy-start(s32[1,8]{1,0:T(1,128)} %param.23) | copy-start | bytes 100
  6.5 15.4 %copy-start.8 = (s32[1,8]{1,0:T(1,128)S(1)}, s32[1,8]{1,0:T(1,128)}, u32[]{:S(2)}) copy-start(s32[1,8]{1,0:T(1,128)} %param.22) | copy-start | bytes 100
  6.5 15.6 %copy-start.5 = (bf16[1,64,128]{2,1,0:T(8,128)(2,1)S(1)}, bf16[1,64,128]{2,1,0:T(8,128)(2,1)}, u32[]{:S(2)}) copy-start(bf16[1,64,128]{2,1,0:T(8,128)(2,1)} %param.17) | copy-start | bytes 49156
  6.5 33.4 %copy-start.6 = (s32[1,8,128]{2,1,0:T(8,128)S(1)}, s32[1,8,128]{2,1,0:T(8,128)}, u32[]{:S(2)}) copy-start(s32[1,8,128]{2,1,0:T(8,128)} %param.21) | copy-start | bytes 12292
  6.5 88.7 %all-gather.2.cloned.1.call-start = ((), (), s32[]{:S(2)}) async-start(), calls=%async_computation.2 | async-start | bytes 8912896 | tf_op jit(solution)/shard_map/all_gather | solution.py:101
  12.2 29.6 %copy-start.4 = (bf16[128,1,192]{0,2,1:T(8,128)(2,1)S(1)}, bf16[128,1,192]{0,2,1:T(8,128)(2,1)}, u32[]{:S(2)}) copy-start(bf16[128,1,192]{0,2,1:T(8,128)(2,1)} %param.16) | copy-start | bytes 147460
  14.7 45.7 %all-to-all-start = ((bf16[16,16,16,128]{3,1,0,2:T(8,128)(2,1)}), bf16[16,16,16,128]{3,1,0,2:T(8,128)(2,1)S(1)}, u32[]{:S(2)}, u32[]{:S(2)}) async-start(bf16[16,16,16,128]{3,1,0,2:T(8,128)(2,1)} %bitcast.193), calls=%async_computation | async-start | bytes 2097152 | tf_op jit(solution)/shard_map/all_to_all | solution.py:139
  21.7 327.2 %reduce-scatter.2.cloned.1.call-start = ((), (), s32[]{:S(2)}) async-start(), calls=%async_computation.3 | async-start | bytes 8912896 | tf_op jit(solution)/shard_map/reduce_scatter | solution.py:158
  95.2 6.5 %copy-start.9 = (f32[16]{0:T(128)S(1)}, f32[16]{0:T(128)}, u32[]{:S(2)}) copy-start(f32[16]{0:T(128)} %multiply_power_fusion) | copy-start | bytes 196
  231.7 15.9 %copy-start.2 = (f32[2048,1,1,1,1,1,64]{0,6,5,4,3,2,1:T(8,128)S(1)}, f32[2048,1,1,1,1,1,64]{0,6,5,4,3,2,1:T(8,128)}, u32[]{:S(2)}) copy-start(f32[2048,1,1,1,1,1,64]{0,6,5,4,3,2,1:T(8,128)} %reshape.624) | copy-start | bytes 1572868
  231.7 15.9 %copy-start.3 = (bf16[1,64,2048]{2,1,0:T(8,128)(2,1)S(1)}, bf16[1,64,2048]{2,1,0:T(8,128)(2,1)}, u32[]{:S(2)}) copy-start(bf16[1,64,2048]{2,1,0:T(8,128)(2,1)} %all_gather.11) | copy-start | bytes 786436
  259.0 89.9 %copy-start.1 = (bf16[1,128,2048]{2,1,0:T(8,128)(2,1)S(1)}, bf16[1,128,2048]{2,1,0:T(8,128)(2,1)}, u32[]{:S(2)}) copy-start(bf16[1,128,2048]{2,1,0:T(8,128)(2,1)} %param.14) | copy-start | bytes 1572868
Sparse Core Ops, SparseCore 0:
  12.3 82.8 all-gather.1
  259.2 89.7 reduce-scatter.1
where the time goes:
time: 361 us; the launch traced here: 358 us
  waiting for transfers between devices  120 us (33%)
  local copies, waits for them, and re-layouts  80.2 us (22%)
  matrix products  64.2 us (18%)
  blocking collectives  35.9 us (10%)
  other arithmetic  31.4 us (9%)
  between operations  13.6 us (4%)
  starting transfers between devices  7.11 us (2%)
  loops' own time  5.54 us (2%)
    reduce_scatter x1, waiting for transfers between devices, per_device(): lax.psum_scatter((jnp.dot(attention, out_rows, preferred_element_type=jnp...  89.9 us
    dynamic_update_slice x24, local copies, waits for them, and re-layouts, per_device(): high_new, total_new, sum_new = lax.map(new_block, block_ids)  32.7 us
    all_gather x1, waiting for transfers between devices, per_device(): piece = lax.all_gather(normed, 'pool', axis=0, tiled=True)  29.9 us
    reduce_sum x8, other arithmetic, partial_attention(): total = jnp.sum(weights.astype(jnp.float32), axis=-1)  20.4 us
    dot_general x8, matrix products, partial_attention(): jnp.einsum('rhe,khe->rhk', queries, keys, preferred_element_type=jnp.floa...  20.4 us
    all_gather x1, blocking collectives, per_device(): lax.all_gather(w_qkv, 'grp', axis=0, tiled=True)  18.7 us
    reshape x4, local copies, waits for them, and re-layouts, partial_attention(): scores = jnp.where(visible[:, None, :], scores, -1e+30)  18 us
    all_gather x1, blocking collectives, per_device(): lax.all_gather(w_out, 'grp', axis=2, tiled=True)  17.2 us
  transfers between devices with their start and end apart: 3, of which 2 were waited for; matrix products, arithmetic and copies ran while one was open for 3% of the time, Pallas kernels for 0%

commit v1 on v0

v1 whole, which is shorter than its diff:
```python
import functools

import jax
import jax.numpy as jnp
from jax import lax
from jax.experimental import pallas as pl
from jax.experimental.pallas import tpu as pltpu
from jax.sharding import PartitionSpec as P

ROT = 32


epsilon = 1e-05


def layer_norm(rows, gain):
    values = rows.astype(jnp.float32)
    centred = values - jnp.mean(values, axis=-1, keepdims=True)
    variance = jnp.mean(centred * centred, axis=-1, keepdims=True)
    return (centred * lax.rsqrt(variance + epsilon) * gain.astype(jnp.float32)).astype(jnp.bfloat16)


def rotate(field, where):
    half = ROT // 2
    frequency = 10000.0 ** (-2.0 * jnp.arange(half, dtype=jnp.float32) / ROT)
    angle = where.astype(jnp.float32)[:, None] * frequency[None, :]
    cosine = jnp.cos(angle)[:, None, :]
    sine = jnp.sin(angle)[:, None, :]
    first = field[..., :half]
    second = field[..., half:ROT]
    return jnp.concatenate(
        [first * cosine - second * sine, second * cosine + first * sine, field[..., ROT:]], axis=-1
    )


def positions(request_lengths, counts, group_tok, block_len):
    ends = jnp.cumsum(request_lengths)
    starts = ends - request_lengths
    token_index = jnp.arange(group_tok, dtype=jnp.int32)
    inside = (token_index[:, None] >= starts[None, :]) & (token_index[:, None] < ends[None, :])
    position = (
        jnp.sum(jnp.where(inside, (counts * block_len - starts)[None, :], 0), axis=-1) + token_index
    )
    return position


LOG2E = 1.4426950408889634


def attention_kernel(
    chunk, span, scale, table_ref, count_ref, length_ref, query_ref, fresh_ref, pool_ref,
    out_ref, key_ref, value_ref
):
    tokens, lanes = query_ref.shape
    head_dim = lanes // 2
    block_len = pool_ref.shape[1]
    requests = table_ref.shape[0]
    per_chunk = chunk // block_len
    factor = scale * LOG2E
    tile = span
    unroll = 8
    block_lane = lax.broadcasted_iota(jnp.int32, (block_len, lanes), 1)
    one = jnp.ones((), jnp.bfloat16)
    nil = jnp.zeros((), jnp.bfloat16)

    def step(carry, query, keys, values, visible):
        highest, acc = carry
        scores = factor * lax.dot_general(
            query, keys, (((1,), (1,)), ((), ())), preferred_element_type=jnp.float32
        )
        if visible is not None:
            scores = jnp.where(visible, scores, -1e30)
        top = jnp.maximum(highest, jnp.max(scores, axis=-1, keepdims=True))
        weights = jnp.exp2(scores - top).astype(jnp.bfloat16)
        acc = acc * jnp.exp2(highest - top) + jnp.dot(
            weights, values, preferred_element_type=jnp.float32
        )
        return top, acc

    def request(r, start):
        length = length_ref[r]
        count = count_ref[r]
        chunks = (count + per_chunk - 1) // per_chunk

        def gather(i, _):
            for u in range(unroll):
                b = i * unroll + u
                block = pool_ref[table_ref[r, jnp.minimum(b, count - 1)]]
                where = pl.ds(pl.multiple_of(b * block_len, block_len), block_len)
                key_ref[where, :] = block
                paired = jnp.where(block_lane < head_dim, one, block)
                value_ref[where, :] = jnp.where(b < count, paired, nil)
            return 0

        lax.fori_loop(0, chunks * (per_chunk // unroll), gather, 0)
        first = start // 16 * 16
        tiles = (start + length - first + tile - 1) // tile

        def one_tile(i, _):
            row = pl.multiple_of(jnp.minimum(first + i * tile, tokens - tile), 16)
            rows = pl.ds(row, tile)
            query = query_ref[rows, :]

            def pooled(j, carry):
                where = pl.ds(pl.multiple_of(j * chunk, chunk), chunk)
                return step(carry, query, key_ref[where, :], value_ref[where, :], None)

            carry = (
                jnp.full((tile, 1), -1e30, jnp.float32),
                jnp.zeros((tile, lanes), jnp.float32),
            )
            carry = lax.fori_loop(0, chunks, pooled, carry)
            own = row + lax.broadcasted_iota(jnp.int32, (tile, span), 0)

            def new(j, carry):
                begin = pl.multiple_of(j * span, span)
                both = fresh_ref[pl.ds(begin, span), :]
                lane = lax.broadcasted_iota(jnp.int32, (span, lanes), 1)
                values = jnp.where(lane < head_dim, one, both)
                other = begin + lax.broadcasted_iota(jnp.int32, (tile, span), 1)
                visible = (other >= start) & (other <= own)
                return step(carry, query, both, values, visible)

            highest, acc = lax.fori_loop(
                start // span, (row + tile + span - 1) // span, new, carry
            )
            result = (acc[:, head_dim:] / acc[:, :head_dim]).astype(jnp.bfloat16)
            place = row + lax.broadcasted_iota(jnp.int32, (tile, head_dim), 0)
            inside = (place >= start) & (place < start + length)
            out_ref[rows, :] = jnp.where(inside, result, out_ref[rows, :])
            return 0

        lax.fori_loop(0, tiles, one_tile, 0)
        return start + length

    lax.fori_loop(0, requests, request, 0)


def attend(query, fresh, pool, table, counts, lengths, chunk=512, span=256):
    tokens, lanes = query.shape
    block_len = pool.shape[1]
    keys = table.shape[1] * block_len
    keys = -(-keys // chunk) * chunk
    head_dim = lanes // 2
    smem = pl.BlockSpec(memory_space=pltpu.SMEM)
    vmem = pl.BlockSpec(memory_space=pltpu.VMEM)
    return pl.pallas_call(
        functools.partial(attention_kernel, chunk, span, head_dim**-0.5),
        out_shape=jax.ShapeDtypeStruct((tokens, head_dim), jnp.bfloat16),
        in_specs=[smem, smem, smem, vmem, vmem, vmem],
        out_specs=vmem,
        scratch_shapes=[
            pltpu.VMEM((keys, lanes), jnp.bfloat16),
            pltpu.VMEM((keys, lanes), jnp.bfloat16),
        ],
        compiler_params=pltpu.CompilerParams(vmem_limit_bytes=24 * 1024 * 1024),
        cost_estimate=pl.CostEstimate(
            flops=2 * tokens * keys * lanes * 2, bytes_accessed=3 * 1024 * 1024,
            transcendentals=tokens * keys,
        ),
        name="attend",
    )(table, counts, lengths, query, fresh, pool)


def per_device(
    tokens, ln_gain, w_qkv, w_out, w_fc, w_proj, pool_kv, block_table, block_count, lengths
):
    holders = lax.axis_size("pool")
    rows_dev = tokens.shape[1]
    group_tok = rows_dev * holders
    local_pool = pool_kv[0]
    blk_dev, block_len, heads_all, paired = local_pool.shape
    head_dim = paired // 2
    pool_blocks = blk_dev * holders
    qkv_weight, out_weight = (
        lax.all_gather(w_qkv, "grp", axis=0, tiled=True),
        lax.all_gather(w_out, "grp", axis=2, tiled=True),
    )
    heads_dev = qkv_weight.shape[1]
    position = positions(lengths[0], block_count[0], group_tok, block_len)
    normed = layer_norm(tokens[0], ln_gain)
    units = w_fc.shape[1]
    piece = lax.all_gather(normed, "pool", axis=0, tiled=True)
    count = piece.shape[0]
    hidden_rows = jax.nn.gelu(
        jnp.dot(piece, w_fc, preferred_element_type=jnp.float32), approximate=True
    ).astype(jnp.bfloat16)
    projected = jnp.einsum("td,dhe->the", piece, qkv_weight, preferred_element_type=jnp.float32)
    query_rows = rotate(projected[..., :head_dim], position)
    key_rows = rotate(projected[..., head_dim : 2 * head_dim], position)
    joined = jnp.concatenate(
        [query_rows, key_rows, projected[..., 2 * head_dim :]], axis=-1
    ).astype(jnp.bfloat16)
    results = jnp.concatenate(
        [hidden_rows, joined.reshape(count, heads_dev * 3 * head_dim)], axis=1
    )
    hidden = results[:, :units]
    joined = results[:, units:].reshape(group_tok, heads_dev, 3 * head_dim)
    query = joined[:, 0, :head_dim]
    query = jnp.concatenate([query, jnp.zeros_like(query)], axis=1)
    fresh = joined[:, 0, head_dim:]
    pooled = lax.all_to_all(local_pool, "pool", split_axis=2, concat_axis=0, tiled=True)
    pooled = pooled.reshape(pool_blocks, block_len, paired)
    attention = attend(query, fresh, pooled, block_table[0], block_count[0], lengths[0])
    attention = attention.reshape(group_tok, heads_dev * head_dim)
    out_rows = out_weight.reshape(heads_dev * head_dim, out_weight.shape[2])
    summed = lax.psum_scatter(
        (
            jnp.dot(attention, out_rows, preferred_element_type=jnp.float32)
            + jnp.dot(hidden, w_proj, preferred_element_type=jnp.float32)
        ).astype(jnp.bfloat16),
        "pool",
        scatter_dimension=0,
        tiled=True,
    ).astype(jnp.float32)
    return (tokens[0].astype(jnp.float32) + summed).astype(jnp.bfloat16)[None]


def solution(mesh):
    in_specs = (
        P("grp", "pool", None),
        P(),
        P("grp", "pool", None),
        P("pool", None, "grp"),
        P(None, "pool"),
        P("pool", None),
        P("grp", "pool", None, None, None),
        P("grp", None, None),
        P("grp", None),
        P("grp", None),
    )
    out_specs = P("grp", "pool", None)
    return jax.shard_map(
        per_device, mesh=mesh, in_specs=in_specs, out_specs=out_specs, check_vma=False
    )
```

time: 361 us -> 280 us (0.78)
  local copies, waits for them, and re-layouts: 80.2 us -> 6.69 us
  Pallas kernels: 0 us -> 34.5 us
  matrix products: 64.2 us -> 33.1 us
  other arithmetic: 31.4 us -> 14.6 us
  waiting for transfers between devices: 120 us -> 134 us
  loops' own time: 5.54 us -> 0 us
    pallas_call x0 -> x1, Pallas kernels: none -> 34.5 us  [attend(): pl.pallas_call(functools.partial(attention_kernel, chunk, span, head_dim...]
    dynamic_update_slice x24 -> x0, local copies, waits for them, and re-layouts: 32.7 us -> none  [per_device(): high_new, total_new, sum_new = lax.map(new_block, block_ids)]
    dot_general x17 -> x0, matrix products: 30.5 us -> none  [the longest x8 20.4 us: partial_attention(): jnp.einsum('rhe,khe->rhk', queries, keys, preferred_element_type=jnp.floa...]
    reshape x6 -> x0, local copies, waits for them, and re-layouts: 21.6 us -> none  [the longest x4 18 us: partial_attention(): scores = jnp.where(visible[:, None, :], scores, -1e+30)]
    reduce_sum x9 -> x1, other arithmetic: 20.5 us -> 0.1 us  [positions(): jnp.sum(jnp.where(inside, (counts * block_len - starts)[None, :], 0), axi...]
    dynamic_slice x24 -> x0, local copies, waits for them, and re-layouts: 12.7 us -> none  [the longest x8 7.47 us: per_device(): high_new, total_new, sum_new = lax.map(new_block, block_ids)]
    all_gather x1, waiting for transfers between devices: 29.9 us -> 38.6 us  [per_device(): piece = lax.all_gather(normed, 'pool', axis=0, tiled=True)]
    another operation x2 -> x0, loops' own time: 5.54 us -> none  [the longest x1 2.95 us: per_device(): highs, totals, sums = lax.map(pool_block, block_ids)]
  transfers between devices with their start and end apart: 3 -> 3, of which waited for: 2 -> 2; matrix products, arithmetic and copies ran while one was open for 3% -> 6% of each run, Pallas kernels for 0% -> 0%
where the time goes in v1:
time: 280 us; the launch traced here: 278 us
  waiting for transfers between devices  134 us (48%)
  blocking collectives  34.5 us (12%)
  Pallas kernels  34.5 us (12%)
  matrix products  33.1 us (12%)
  other arithmetic  14.6 us (5%)
  between operations  13.5 us (5%)
  starting transfers between devices  7.11 us (3%)
  local copies, waits for them, and re-layouts  6.69 us (2%)
    reduce_scatter x1, waiting for transfers between devices, per_device(): lax.psum_scatter((jnp.dot(attention, out_rows, preferred_element_type=jnp...  95.1 us
    all_gather x1, waiting for transfers between devices, per_device(): piece = lax.all_gather(normed, 'pool', axis=0, tiled=True)  38.6 us
    pallas_call x1, Pallas kernels, attend(): pl.pallas_call(functools.partial(attention_kernel, chunk, span, head_dim...  34.5 us
    all_gather x1, blocking collectives, per_device(): lax.all_gather(w_qkv, 'grp', axis=0, tiled=True)  18.7 us
    all_gather x1, blocking collectives, per_device(): lax.all_gather(w_out, 'grp', axis=2, tiled=True)  15.8 us
    dot_general x1, matrix products, per_device(): jnp.dot(hidden, w_proj, preferred_element_type=jnp.float32)  15.7 us
    dot_general x1, matrix products, per_device(): jnp.dot(attention, out_rows, preferred_element_type=jnp.float32)  11.5 us
    all_to_all x1, starting transfers between devices, per_device(): lax.all_to_all(local_pool, 'pool', split_axis=2, concat_axis=0, tiled=True)  7.03 us
  transfers between devices with their start and end apart: 3, of which 2 were waited for; matrix products, arithmetic and copies ran while one was open for 6% of the time, Pallas kernels for 0%

profile of v1, /device:TPU:160, one launch (start us, length us, event | category | flops | bytes accessed | tf_op | source)
XLA Modules:
  0.0 277.8 jit_solution(1824032372011711579)
XLA Ops:
  6.5 0.0 copy-start
  6.5 0.0 copy-start.5
  6.5 0.0 copy-start.4
  6.5 0.0 copy-start.9
  6.5 0.0 copy-start.8
  6.5 0.0 all-gather.2.cloned.1.call-start
  6.6 1.3 convert_reduce_fusion
  7.9 1.3 fusion.26
  9.3 0.7 convert_element_type.44
  10.0 2.2 fusion.28
  12.2 0.0 all-gather.2.cloned.1.call-update
  12.2 2.5 copy.22
  14.7 7.0 %all-to-all-start = ((bf16[16,16,16,128]{3,1,0,2:T(8,128)(2,1)}), bf16[16,16,16,128]{3,1,0,2:T(8,128)(2,1)S(1)}, u32[]{:S(2)}, u32[]{:S(2)}) async-start(bf16[16,16,16,128]{3,1,0,2:T(8,128)(2,1)} %bitcast.69), calls=%async_computation | async-start | bytes 2097152 | tf_op jit(solution)/shard_map/all_to_all | solution.py:202
  21.7 0.0 reduce-scatter.2.cloned.1.call-start
  21.8 0.0 copy-done.5
  21.8 0.2 reduce-window.4
  22.0 0.0 copy-done.4
  22.0 0.1 select_reduce_fusion
  22.1 0.0 copy-done.9
  22.1 15.8 %all_gather.11 = bf16[1,64,2048]{2,1,0:T(8,128)(2,1)S(1)} all-gather(bf16[1,64,128]{2,1,0:T(8,128)(2,1)S(1)} %copy-done.9), channel_id=1, replica_groups=mesh['grp'=16,'pool'=16] {'grp'}, dimensions={2}, use_global_device_ids=true | all-gather | bytes 278528 | tf_op jit(solution)/shard_map/all_gather | solution.py:177
  37.9 0.0 copy-done.8
  37.9 18.7 %all_gather.10 = bf16[2048,1,192]{0,2,1:T(8,128)(2,1)} all-gather(bf16[128,1,192]{0,2,1:T(8,128)(2,1)S(1)} %copy-done.8), channel_id=1, replica_groups=mesh['grp'=16,'pool'=16] {'grp'}, dimensions={0}, use_global_device_ids=true | all-gather | bytes 835584 | tf_op jit(solution)/shard_map/all_gather | solution.py:176
  56.6 38.6 %all-gather.2.cloned.1.call-done = bf16[2048,2048]{1,0:T(8,128)(2,1)} async-done(((bf16[128,2048]{1,0:T(8,128)(2,1)}), bf16[2048,2048]{1,0:T(8,128)(2,1)}) %all-gather.2.cloned.1.call-update) | async-done | bytes 8388624 | tf_op jit(solution)/shard_map/all_gather | solution.py:183
  95.2 5.9 %fusion.47 = (bf16[2048,1,192]{2,0,1:T(8,128)(2,1)S(1)}, f32[2048,1,192]{2,0,1:T(8,128)S(1)}) fusion(bf16[2048,2048]{1,0:T(8,128)(2,1)} %all-gather.2.cloned.1.call-done, bf16[2048,1,192]{0,2,1:T(8,128)(2,1)} %all_gather.10), kind=kOutput, calls=%fused_computation.65 | convolution fusion | flops 1611005952 | bytes 11534336 | tf_op jit(solution)/shard_map/td,dhe->the/dot_general | solution.py:188
  101.1 0.2 slice.45
  101.3 0.2 slice.42
  101.5 5.0 %fusion.35 = (bf16[2048,1,16]{2,0,1:T(8,128)(2,1)S(1)}, bf16[2048,1,16]{2,0,1:T(8,128)(2,1)S(1)}, bf16[2048,1,16]{2,0,1:T(8,128)(2,1)S(1)}, bf16[2048,1,16]{2,0,1:T(8,128)(2,1)S(1)}) fusion(f32[2048,1,192]{2,0,1:T(8,128)S(1)} %get-tuple-element.12, f32[2048]{0:T(1024)S(1)} %add_convert_fusion.1, f32[16]{0:T(128)S(1)} %multiply_power_fusion), kind=kLoop, calls=%fused_computation.41 | loop fusion | flops 557056 | bytes 794688 | tf_op jit(solution)/shard_map/convert.3
  106.6 0.0 copy-start.6
  106.6 0.5 maximum_bitcast_fusion
  107.1 0.9 concatenate.21.query_ref
  108.0 1.3 maximum_bitcast_fusion.1.fresh_ref
  109.3 0.0 all-to-all-done
  109.3 0.0 copy-done.6
  109.3 0.0 copy-start.2
  109.3 1.0 copy-done.2
  110.3 0.0 copy-start.3
  110.3 1.0 copy-done.3
  111.4 34.5 %attend.1 = bf16[2048,64]{1,0:T(8,128)(2,1)S(1)} custom-call(s32[8,128]{1,0:T(8,128)S(1)} %bitcast.68, s32[8]{0:T(128)S(1)} %bitcast.65, s32[8]{0:T(128)S(1)} %bitcast.67, bf16[2048,128]{1,0:T(8,128)(2,1)S(1)} %copy-done.2, bf16[2048,128]{1,0:T(8,128)(2,1)S(1)} %copy-done.3, bf16[256,16,128]{2,1,0:T(8,128)(2,1)S(1)} %bitcast.64), custom_call_target="tpu_custom_call" | custom-call | flops 2147483648 | bytes 3145728 | tf_op jit(solution)/shard_map/attend/pallas_call | solution.py:147
  145.9 0.0 copy-start.1
  145.9 0.8 copy-done.1
  146.7 0.0 copy-done
  146.7 15.7 %fusion.8 = f32[2048,2048]{1,0:T(8,128)} fusion(bf16[512,2048]{1,0:T(8,128)(2,1)S(1)} %copy-done, bf16[2048,2048]{1,0:T(8,128)(2,1)} %all-gather.2.cloned.1.call-done, bf16[2048,512]{1,0:T(8,128)(2,1)} %param.14), kind=kOutput, calls=%fused_computation.11 | convolution fusion | flops 8599371776 | bytes 29360128 | tf_op jit(solution)/shard_map/dot_general | solution.py:210
  162.4 11.5 %add_convert_fusion = bf16[2048,2048]{1,0:T(8,128)(2,1)} fusion(f32[2048,2048]{1,0:T(8,128)} %fusion.8, bf16[2048,64]{1,0:T(8,128)(2,1)} %copy-done.1, bf16[1,64,2048]{2,1,0:T(8,128)(2,1)S(1)} %all_gather.11), kind=kOutput, calls=%fused_computation | convolution fusion | flops 545259520 | bytes 25690112 | tf_op jit(solution)/shard_map/dot_general | solution.py:209
  173.9 0.0 copy-start.7
  173.9 0.0 reduce-scatter.2.cloned.1.call-update
  173.9 95.1 %reduce-scatter.2.cloned.1.call-done = bf16[128,2048]{1,0:T(8,128)(2,1)} async-done(((bf16[2048,2048]{1,0:T(8,128)(2,1)}), bf16[128,2048]{1,0:T(8,128)(2,1)}) %reduce-scatter.2.cloned.1.call-update) | async-done | bytes 524304 | tf_op jit(solution)/shard_map/reduce_scatter | solution.py:207
  269.0 0.0 copy-done.7
  269.0 2.0 fusion.39
  (5 shorter events, 0.0 us)
Async XLA Ops:
  6.5 140.2 %copy-start = (bf16[512,2048]{1,0:T(8,128)(2,1)S(1)}, bf16[512,2048]{1,0:T(8,128)(2,1)}, u32[]{:S(2)}) copy-start(bf16[512,2048]{1,0:T(8,128)(2,1)} %param.15) | copy-start | bytes 6291460
  6.5 15.2 %copy-start.5 = (s32[1,8]{1,0:T(1,128)S(1)}, s32[1,8]{1,0:T(1,128)}, u32[]{:S(2)}) copy-start(s32[1,8]{1,0:T(1,128)} %param.19) | copy-start | bytes 100
  6.5 15.4 %copy-start.4 = (s32[1,8]{1,0:T(1,128)S(1)}, s32[1,8]{1,0:T(1,128)}, u32[]{:S(2)}) copy-start(s32[1,8]{1,0:T(1,128)} %param.18) | copy-start | bytes 100
  6.5 15.5 %copy-start.9 = (bf16[1,64,128]{2,1,0:T(8,128)(2,1)S(1)}, bf16[1,64,128]{2,1,0:T(8,128)(2,1)}, u32[]{:S(2)}) copy-start(bf16[1,64,128]{2,1,0:T(8,128)(2,1)} %param.13) | copy-start | bytes 49156
  6.5 31.4 %copy-start.8 = (bf16[128,1,192]{0,2,1:T(8,128)(2,1)S(1)}, bf16[128,1,192]{0,2,1:T(8,128)(2,1)}, u32[]{:S(2)}) copy-start(bf16[128,1,192]{0,2,1:T(8,128)(2,1)} %param.12) | copy-start | bytes 147460
  6.5 88.7 %all-gather.2.cloned.1.call-start = ((), (), s32[]{:S(2)}) async-start(), calls=%async_computation.2 | async-start | bytes 8912896 | tf_op jit(solution)/shard_map/all_gather | solution.py:183
  14.7 94.6 %all-to-all-start = ((bf16[16,16,16,128]{3,1,0,2:T(8,128)(2,1)}), bf16[16,16,16,128]{3,1,0,2:T(8,128)(2,1)S(1)}, u32[]{:S(2)}, u32[]{:S(2)}) async-start(bf16[16,16,16,128]{3,1,0,2:T(8,128)(2,1)} %bitcast.69), calls=%async_computation | async-start | bytes 2097152 | tf_op jit(solution)/shard_map/all_to_all | solution.py:202
  21.7 247.3 %reduce-scatter.2.cloned.1.call-start = ((), (), s32[]{:S(2)}) async-start(), calls=%async_computation.3 | async-start | bytes 8912896 | tf_op jit(solution)/shard_map/reduce_scatter | solution.py:207
  106.6 2.7 copy-start.6
  109.3 1.0 copy-start.2
  110.3 1.0 copy-start.3
  145.9 0.8 copy-start.1
  173.9 95.1 %copy-start.7 = (bf16[1,128,2048]{2,1,0:T(8,128)(2,1)S(1)}, bf16[1,128,2048]{2,1,0:T(8,128)(2,1)}, u32[]{:S(2)}) copy-start(bf16[1,128,2048]{2,1,0:T(8,128)(2,1)} %param.10) | copy-start | bytes 1572868
Sparse Core Ops, SparseCore 0:
  12.3 82.8 all-gather.1
  174.0 94.9 reduce-scatter.1

commit v2 on v1

v2 whole, which is shorter than its diff:
```python
import functools

import jax
import jax.numpy as jnp
from jax import lax
from jax.experimental import pallas as pl
from jax.experimental.pallas import tpu as pltpu
from jax.sharding import Mesh
from jax.sharding import PartitionSpec as P

ROT = 32
LOG2E = 1.4426950408889634
MIB = 1024 * 1024
epsilon = 1e-05


def layer_norm(rows, gain):
    values = rows.astype(jnp.float32)
    centred = values - jnp.mean(values, axis=-1, keepdims=True)
    variance = jnp.mean(centred * centred, axis=-1, keepdims=True)
    return (centred * lax.rsqrt(variance + epsilon) * gain.astype(jnp.float32)).astype(jnp.bfloat16)


def rotation_tables(request_lengths, counts, first_token, tokens, block_len, lanes):
    half = ROT // 2
    ends = jnp.cumsum(request_lengths)
    starts = ends - request_lengths
    index = first_token + jnp.arange(tokens, dtype=jnp.int32)
    inside = (index[:, None] >= starts[None, :]) & (index[:, None] < ends[None, :])
    position = (
        jnp.sum(jnp.where(inside, (counts * block_len - starts)[None, :], 0), axis=-1) + index
    )
    frequency = 10000.0 ** (-2.0 * jnp.arange(half, dtype=jnp.float32) / ROT)
    lane = jnp.arange(lanes, dtype=jnp.int32)
    spread = jnp.where(lane < ROT, jnp.tile(frequency, lanes // half), 0.0)
    angle = position.astype(jnp.float32)[:, None] * spread[None, :]
    sine = jnp.sin(angle)
    return jnp.cos(angle), jnp.where(lane[None, :] < half, -sine, sine)


def qkv_kernel(
    place_ref, own_ref, right_ref, low_ref, high_ref, left_ref, weight_ref, cos_ref, sin_ref,
    rows_ref, sent_ref
):
    x, y = place_ref[0], place_ref[1]
    ring = sent_ref.shape[0]
    part = own_ref.shape[0]
    tokens, lanes = cos_ref.shape
    head = lanes // 2

    def put(piece, step, offset):
        begin = pl.multiple_of(lax.rem(x + step, ring) * part + offset, 16)
        rows_ref[pl.ds(begin, piece.shape[0]), :] = piece[...]

    put(own_ref, 0, 0)
    put(right_ref, 1, 0)
    put(low_ref, 2, 0)
    put(high_ref, 2, part // 2)
    put(left_ref, 3, 0)
    lane = lax.broadcasted_iota(jnp.int32, (tokens, lanes), 1)

    def rotated(field):
        other = jnp.where(
            lane < ROT // 2, pltpu.roll(field, lanes - ROT // 2, 1), pltpu.roll(field, ROT // 2, 1)
        )
        return field * cos_ref[...] + other * sin_ref[...]

    def product(begin, size):
        weight = jnp.concatenate(
            [weight_ref[g, begin : begin + size, :] for g in range(weight_ref.shape[0])], axis=1
        )
        return lax.dot_general(
            rows_ref[...], weight, (((1,), (1,)), ((), ())), preferred_element_type=jnp.float32
        )

    for pair in range(ring // 2):
        both = product(pair * 2 * lanes, 2 * lanes)
        for k in range(2):
            target = lax.rem(y + 2 * pair + k, ring)
            field = rotated(both[:, k * lanes : (k + 1) * lanes])
            sent_ref[target, :tokens, :] = field.astype(jnp.bfloat16)
    queries = product(ring * lanes, ring * head)
    for d in range(ring):
        field = queries[:, d // 2 * lanes : (d // 2 + 1) * lanes]
        if d % 2:
            field = pltpu.roll(field, head, 1)
        field = rotated(field)
        top, bottom = field[: tokens // 2], pltpu.roll(field[tokens // 2 :], head, 1)
        folded = jnp.where(lane[: tokens // 2] < head, top, bottom)
        sent_ref[lax.rem(y + d, ring), tokens:, :] = folded.astype(jnp.bfloat16)


def attention_kernel(
    chunk, span, scale, table_ref, count_ref, length_ref, sent_ref, pool_ref, out_ref,
    query_ref, fresh_ref, result_ref, key_ref, value_ref
):
    tokens, lanes = query_ref.shape
    head = lanes // 2
    ring = sent_ref.shape[0]
    part = tokens // ring
    block_len = pool_ref.shape[1]
    requests = table_ref.shape[0]
    per_chunk = chunk // block_len
    factor = scale * LOG2E
    tile = span
    unroll = 8
    block_lane = lax.broadcasted_iota(jnp.int32, (block_len, lanes), 1)
    fold_lane = lax.broadcasted_iota(jnp.int32, (part // 2, lanes), 1)
    one = jnp.ones((), jnp.bfloat16)
    nil = jnp.zeros((), jnp.bfloat16)

    for i in range(ring):
        fresh_ref[i * part : (i + 1) * part, :] = sent_ref[i, :part, :]
        folded = sent_ref[i, part:, :].astype(jnp.float32)
        for k in range(2):
            unfolded = folded if k == 0 else pltpu.roll(folded, head, 1)
            begin = i * part + k * (part // 2)
            query_ref[begin : begin + part // 2, :] = jnp.where(
                fold_lane < head, unfolded, 0.0
            ).astype(jnp.bfloat16)

    def step(carry, query, keys, values, visible):
        highest, acc = carry
        scores = factor * lax.dot_general(
            query, keys, (((1,), (1,)), ((), ())), preferred_element_type=jnp.float32
        )
        if visible is not None:
            scores = jnp.where(visible, scores, -1e30)
        top = jnp.maximum(highest, jnp.max(scores, axis=-1, keepdims=True))
        weights = jnp.exp2(scores - top).astype(jnp.bfloat16)
        acc = acc * jnp.exp2(highest - top) + jnp.dot(
            weights, values, preferred_element_type=jnp.float32
        )
        return top, acc

    def request(r, start):
        length = length_ref[r]
        count = count_ref[r]
        chunks = (count + per_chunk - 1) // per_chunk

        def gather(i, _):
            for u in range(unroll):
                b = i * unroll + u
                block = pool_ref[table_ref[r, jnp.minimum(b, count - 1)]]
                where = pl.ds(pl.multiple_of(b * block_len, block_len), block_len)
                key_ref[where, :] = block
                paired = jnp.where(block_lane < head, one, block)
                value_ref[where, :] = jnp.where(b < count, paired, nil)
            return 0

        lax.fori_loop(0, chunks * (per_chunk // unroll), gather, 0)
        first = start // 16 * 16
        tiles = (start + length - first + tile - 1) // tile

        def one_tile(i, _):
            row = pl.multiple_of(jnp.minimum(first + i * tile, tokens - tile), 16)
            rows = pl.ds(row, tile)
            query = query_ref[rows, :]

            def pooled(j, carry):
                where = pl.ds(pl.multiple_of(j * chunk, chunk), chunk)
                return step(carry, query, key_ref[where, :], value_ref[where, :], None)

            carry = (
                jnp.full((tile, 1), -1e30, jnp.float32),
                jnp.zeros((tile, lanes), jnp.float32),
            )
            carry = lax.fori_loop(0, chunks, pooled, carry)
            own = row + lax.broadcasted_iota(jnp.int32, (tile, span), 0)

            def new(j, carry):
                begin = pl.multiple_of(j * span, span)
                both = fresh_ref[pl.ds(begin, span), :]
                lane = lax.broadcasted_iota(jnp.int32, (span, lanes), 1)
                values = jnp.where(lane < head, one, both)
                other = begin + lax.broadcasted_iota(jnp.int32, (tile, span), 1)
                visible = (other >= start) & (other <= own)
                return step(carry, query, both, values, visible)

            highest, acc = lax.fori_loop(
                start // span, (row + tile + span - 1) // span, new, carry
            )
            result = (acc / pltpu.roll(acc, head, 1)).astype(jnp.bfloat16)
            place = row + lax.broadcasted_iota(jnp.int32, (tile, lanes), 0)
            inside = (place >= start) & (place < start + length)
            result_ref[rows, :] = jnp.where(inside, result, result_ref[rows, :])
            return 0

        lax.fori_loop(0, tiles, one_tile, 0)
        return start + length

    lax.fori_loop(0, requests, request, 0)
    for i in range(ring):
        top = result_ref[i * part : i * part + part // 2, :].astype(jnp.float32)
        bottom = result_ref[i * part + part // 2 : (i + 1) * part, :].astype(jnp.float32)
        out_ref[i] = jnp.where(fold_lane < head, pltpu.roll(top, head, 1), bottom).astype(
            jnp.bfloat16
        )


def gelu(value):
    return jax.nn.gelu(value, approximate=True).astype(jnp.bfloat16)


def mix_kernel(
    place_ref, rows_ref, fc_ref, proj_ref,
    fc_up_ref, fc_up2_ref, proj_up_ref, proj_up2_ref,
    fc_down_ref, fc_down2_ref, proj_down_ref, proj_down2_ref,
    gathered_ref, heads_ref, out_ref, total_ref, hidden_ref
):
    x, core = place_ref[0], place_ref[2]
    tokens, width = rows_ref.shape
    units = fc_ref.shape[1]
    ring, part, _ = out_ref.shape
    groups, _, lanes = gathered_ref.shape
    head = lanes // 2
    stripe = 512

    def dot(a, b):
        return jnp.dot(a, b, preferred_element_type=jnp.float32)

    def add(columns, value, first=False):
        total_ref[:, columns] = value if first else total_ref[:, columns] + value

    def stripes(body):
        @pl.loop(0, width // stripe)
        def _(i):
            body(pl.ds(pl.multiple_of(i * stripe, stripe), stripe))

    hidden_ref[...] = gelu(dot(rows_ref[...], fc_ref[...]))
    stripes(lambda c: add(c, dot(hidden_ref[...], proj_ref[:, c]), True))

    for fc_a, fc_b, proj_a, proj_b in (
        (fc_up_ref, fc_up2_ref, proj_up_ref, proj_up2_ref),
        (fc_down_ref, fc_down2_ref, proj_down_ref, proj_down2_ref),
    ):
        def half(size, which):
            return pl.ds(pl.multiple_of(which * (size // 2), size // 2), size // 2)

        hidden_ref[...] = gelu(
            dot(rows_ref[:, half(width, core)], fc_a[...])
            + dot(rows_ref[:, half(width, 1 - core)], fc_b[...])
        )
        stripes(
            lambda c, proj_a=proj_a, proj_b=proj_b: add(
                c,
                dot(hidden_ref[:, half(units, core)], proj_a[:, c])
                + dot(hidden_ref[:, half(units, 1 - core)], proj_b[:, c]),
            )
        )

    begin = ring * head
    blocks = units // lanes
    fc = jnp.concatenate(
        [
            jnp.concatenate(
                [
                    gathered_ref[g, begin + b * lanes : begin + (b + 1) * lanes, :]
                    for b in range(blocks)
                ],
                axis=1,
            )
            for g in range(groups)
        ],
        axis=0,
    )
    hidden_ref[...] = gelu(dot(rows_ref[...], fc))
    begin = begin + units

    fold_lane = lax.broadcasted_iota(jnp.int32, (tokens // 2, lanes), 1)
    sides = ([], [])
    for i in range(0, ring, 2):
        a, b = heads_ref[i].astype(jnp.float32), heads_ref[i + 1].astype(jnp.float32)
        sides[0].append(jnp.where(fold_lane < head, a, pltpu.roll(b, head, 1)))
        sides[1].append(jnp.where(fold_lane < head, pltpu.roll(a, head, 1), b))
    attention = jnp.concatenate(
        [jnp.concatenate(side, axis=1) for side in sides], axis=0
    ).astype(jnp.bfloat16)

    per = stripe // lanes
    for i in range(groups // per):
        weights = [
            jnp.concatenate(
                [gathered_ref[i * per + g, rows, :] for g in range(per)], axis=1
            )
            for rows in (slice(begin, begin + units), slice(0, ring * head))
        ]
        columns = slice(i * stripe, (i + 1) * stripe)
        total = (
            total_ref[:, columns] + dot(hidden_ref[...], weights[0]) + dot(attention, weights[1])
        )
        total_ref[:, columns] = total
    for step in range(ring):
        source = pl.ds(pl.multiple_of(lax.rem(x + step, ring) * part, part), part)
        out_ref[step] = total_ref[source, :].astype(jnp.bfloat16)


def call(kernel, name, out_shape, smem, vmem, operands, scratch, limit, flops):
    specs = [pl.BlockSpec(memory_space=pltpu.SMEM)] * smem
    specs += [pl.BlockSpec(memory_space=pltpu.VMEM)] * vmem
    several = isinstance(out_shape, (tuple, list))
    spec = pl.BlockSpec(memory_space=pltpu.VMEM)
    return pl.pallas_call(
        kernel,
        out_shape=out_shape,
        in_specs=specs,
        out_specs=[spec] * len(out_shape) if several else spec,
        scratch_shapes=scratch,
        compiler_params=pltpu.CompilerParams(vmem_limit_bytes=limit * MIB),
        cost_estimate=pl.CostEstimate(flops=flops, bytes_accessed=4 * MIB, transcendentals=0),
        name=name,
    )(*operands)


def per_device(
    tokens, ln_gain, w_qkv, w_out, w_fc, w_proj, pool_kv, block_table, block_count, lengths
):
    bf16 = jnp.bfloat16
    ring = lax.axis_size("x")
    groups = lax.axis_size("z") * lax.axis_size("core")
    x, y = lax.axis_index("x"), lax.axis_index("y")
    core = lax.axis_index("core")
    group = lax.axis_index("z") * lax.axis_size("core") + core
    place = jnp.stack([x, y, core]).astype(jnp.int32)
    up = [(i, (i + 1) % ring) for i in range(ring)]
    down = [(i, (i - 1) % ring) for i in range(ring)]
    across = [(i, (i + 2) % ring) for i in range(ring)]
    swap = [(0, 1), (1, 0)]

    own = tokens[0]
    part, width = own.shape
    row_tok = part * ring
    group_tok = row_tok * ring
    local_pool = pool_kv[0]
    blk_dev, block_len, _, lanes = local_pool.shape
    pool_blocks = blk_dev * ring * ring
    head = lanes // 2
    units = w_fc.shape[1]
    slab = width // groups

    with jax.named_scope("small_weights"):
        small = jnp.concatenate([w_qkv[:, 0, :].T, w_out[0]], axis=0)
        slices = [
            small,
            lax.ppermute(small, "y", down),
            lax.ppermute(small, "y", across),
            lax.ppermute(small, "y", up),
        ]
        packed = jnp.concatenate(
            [s[head : 3 * head] for s in slices] + [s[:head] for s in slices], axis=0
        )
        qkv_weight = lax.all_gather(packed, ("z", "core"), axis=0, tiled=False)

    normed = layer_norm(own, ln_gain)
    with jax.named_scope("gather_tokens"):
        left = lax.ppermute(normed, "x", up)
        right = lax.ppermute(normed, "x", down)
        low = lax.ppermute(left[: part // 2], "x", up)
        high = lax.ppermute(right[part // 2 :], "x", down)

    with jax.named_scope("far_weights"):
        fc_slab = lax.dynamic_slice_in_dim(w_fc, group * slab, slab, 0)
        fc_slab = fc_slab.reshape(slab, units // lanes, lanes).transpose(1, 0, 2).reshape(-1, lanes)
        proj_slab = lax.dynamic_slice_in_dim(w_proj, group * slab, slab, 1)
        far = lax.ppermute(jnp.concatenate([fc_slab, proj_slab], axis=0), "y", across)
        outs = jnp.stack([s[3 * head :] for s in slices])
        outs = jnp.roll(outs, y, axis=0).reshape(ring * head, lanes)
        gathered = lax.all_gather(
            jnp.concatenate([outs, far], axis=0), ("z", "core"), axis=0, tiled=False
        )

    with jax.named_scope("near_weights"):
        fc_half = lax.dynamic_slice_in_dim(w_fc, core * (width // 2), width // 2, 0)
        proj_half = lax.dynamic_slice_in_dim(w_proj, core * (units // 2), units // 2, 0)
        near = []
        for way in (up, down):
            for half in (fc_half, proj_half):
                first = lax.ppermute(half, "y", way)
                near += [first, lax.ppermute(first, "core", swap)]

    pooled = lax.all_to_all(local_pool, ("y", "x"), split_axis=2, concat_axis=0, tiled=True)
    pooled = pooled.reshape(pool_blocks, block_len, lanes)

    cosine, sine = rotation_tables(
        lengths[0], block_count[0], y * row_tok, row_tok, block_len, lanes
    )
    payload = row_tok + row_tok // 2
    rows, sent = call(
        qkv_kernel, "qkv",
        (
            jax.ShapeDtypeStruct((row_tok, width), bf16),
            jax.ShapeDtypeStruct((ring, payload, lanes), bf16),
        ),
        1, 8, (place, normed, right, low, high, left, qkv_weight, cosine, sine),
        (), 40, 2 * row_tok * width * 3 * head * ring,
    )
    received = lax.all_to_all(sent, "y", split_axis=0, concat_axis=0, tiled=True)

    keys = block_table.shape[2] * block_len
    heads = call(
        functools.partial(attention_kernel, 512, 256, head**-0.5), "attend",
        jax.ShapeDtypeStruct((ring, row_tok // 2, lanes), bf16),
        3, 2, (block_table[0], block_count[0], lengths[0], received, pooled),
        [
            pltpu.VMEM((group_tok, lanes), bf16),
            pltpu.VMEM((group_tok, lanes), bf16),
            pltpu.VMEM((group_tok, lanes), bf16),
            pltpu.VMEM((keys, lanes), bf16),
            pltpu.VMEM((keys, lanes), bf16),
        ],
        24, 4 * group_tok * keys * lanes,
    )
    heads = lax.all_to_all(heads, "y", split_axis=0, concat_axis=0, tiled=True)

    partial = call(
        mix_kernel, "mix", jax.ShapeDtypeStruct((ring, part, width), bf16),
        1, 13, (place, rows, w_fc, w_proj, *near, gathered, heads),
        [pltpu.VMEM((row_tok, width), jnp.float32), pltpu.VMEM((row_tok, units), bf16)],
        48, 4 * row_tok * width * units * ring,
    )

    with jax.named_scope("reduce_tokens"):
        half = part // 2
        from_left = lax.ppermute(partial[2, :half], "x", up)
        from_right = lax.ppermute(partial[2, half:], "x", down)

        def plus(a, b):
            return (a.astype(jnp.float32) + b.astype(jnp.float32)).astype(bf16)

        to_right = jnp.concatenate([plus(partial[1, :half], from_left), partial[1, half:]], axis=0)
        to_left = jnp.concatenate([partial[3, :half], plus(partial[3, half:], from_right)], axis=0)
        a = lax.ppermute(to_right, "x", up).astype(jnp.float32)
        b = lax.ppermute(to_left, "x", down).astype(jnp.float32)
    summed = partial[0].astype(jnp.float32) + a + b
    return (own.astype(jnp.float32) + summed).astype(bf16)[None]


def solution(mesh):
    grid = Mesh(mesh.devices.reshape(8, 2, 4, 4), ("z", "core", "y", "x"))
    grp, pool = ("z", "core"), ("y", "x")
    in_specs = (
        P(grp, pool, None),
        P(),
        P(grp, pool, None),
        P(pool, None, grp),
        P(None, pool),
        P(pool, None),
        P(grp, pool, None, None, None),
        P(grp, None, None),
        P(grp, None),
        P(grp, None),
    )
    return jax.shard_map(
        per_device, mesh=grid, in_specs=in_specs, out_specs=P(grp, pool, None), check_vma=False
    )
```

time: 280 us -> 226 us (0.81)
  waiting for transfers between devices: 134 us -> 73.1 us
  matrix products: 33.1 us -> 0 us
  starting transfers between devices: 7.11 us -> 34.9 us
  Pallas kernels: 34.5 us -> 61.8 us
  blocking collectives: 34.5 us -> 15.6 us
  local copies, waits for them, and re-layouts: 6.69 us -> 18.8 us
  other arithmetic: 14.6 us -> 5.2 us
    reduce_scatter x1 -> x0, waiting for transfers between devices: 95.1 us -> none  [per_device(): lax.psum_scatter((jnp.dot(attention, out_rows, preferred_element_type=jnp...]
    ppermute x0 -> x20, waiting for transfers between devices: none -> 65.9 us  [the longest x4 30.4 us: per_device(): first = lax.ppermute(half, 'y', way)]
    all_gather x1 -> x2, waiting for transfers between devices: 38.6 us -> 0.01 us  [the longest x1 0.01 us: per_device(): qkv_weight = lax.all_gather(packed, ('z', 'core'), axis=0, tiled=False)]
    all_gather x2 -> x0, blocking collectives: 34.5 us -> none  [the longest x1 18.7 us: per_device(): lax.all_gather(w_qkv, 'grp', axis=0, tiled=True)]
    dot_general x3 -> x0, matrix products: 33.1 us -> none  [the longest x1 15.7 us: per_device(): jnp.dot(hidden, w_proj, preferred_element_type=jnp.float32)]
    pallas_call x1 -> x3, Pallas kernels: 34.5 us -> 61.8 us  [call(): pl.pallas_call(kernel, out_shape=out_shape, in_specs=specs, out_specs=[sp...]
    ppermute x0 -> x20, starting transfers between devices: none -> 25.5 us  [the longest x4 5.57 us: per_device(): first = lax.ppermute(half, 'y', way)]
    all_to_all x0 -> x1, blocking collectives: none -> 15.6 us  [per_device(): lax.all_to_all(sent, 'y', split_axis=0, concat_axis=0, tiled=True)]
  transfers between devices with their start and end apart: 3 -> 24, of which waited for: 2 -> 11; matrix products, arithmetic and copies ran while one was open for 6% -> 5% of each run, Pallas kernels for 0% -> 18%
where the time goes in v2:
time: 226 us; the launch traced here: 223 us
  waiting for transfers between devices  73.1 us (32%)
  Pallas kernels  61.8 us (27%)
  starting transfers between devices  34.9 us (15%)
  local copies, waits for them, and re-layouts  18.8 us (8%)
  blocking collectives  15.6 us (7%)
  between operations  13.8 us (6%)
  other arithmetic  5.2 us (2%)
    pallas_call x3, Pallas kernels, call(): pl.pallas_call(kernel, out_shape=out_shape, in_specs=specs, out_specs=[sp...  61.8 us
    ppermute x4, waiting for transfers between devices, per_device(): first = lax.ppermute(half, 'y', way)  30.4 us
    all_to_all x1, blocking collectives, per_device(): lax.all_to_all(sent, 'y', split_axis=0, concat_axis=0, tiled=True)  15.6 us
    unnamed x52, local copies, waits for them, and re-layouts  10.6 us
    ppermute x1, waiting for transfers between devices, per_device(): low = lax.ppermute(left[:part // 2], 'x', up)  9.27 us
    ppermute x1, waiting for transfers between devices, per_device(): b = lax.ppermute(to_left, 'x', down).astype(jnp.float32)  8.95 us
    all_to_all x1, waiting for transfers between devices, per_device(): heads = lax.all_to_all(heads, 'y', split_axis=0, concat_axis=0, tiled=True)  7.15 us
    ppermute x1, waiting for transfers between devices, per_device(): lax.ppermute(jnp.concatenate([fc_slab, proj_slab], axis=0), 'y', across)  6.54 us
  transfers between devices with their start and end apart: 24, of which 11 were waited for; matrix products, arithmetic and copies ran while one was open for 5% of the time, Pallas kernels for 18%

profile of v2, /device:TPU:160, one launch (start us, length us, event | category | flops | bytes accessed | tf_op | source)
XLA Modules:
  0.0 223.1 jit_solution(8706686708619232957)
XLA Ops:
  6.5 0.9 pad_maximum_fusion.4
  7.4 1.6 collective-permute-start.6
  9.0 2.9 %collective-permute-start.5 = (bf16[256,128]{1,0:T(8,128)(2,1)S(1)}, bf16[256,128]{1,0:T(8,128)(2,1)S(1)}, u32[]{:S(2)}, u32[]{:S(2)}) collective-permute-start(bf16[256,128]{1,0:T(8,128)(2,1)S(1)} %pad_maximum_fusion.4), channel_id=1, source_target_pairs={{0,8},{4,12},{8,0},{12,4},{1,9},{5,13},{9,1},{13,5},{2,10},{6,14},... | collective-permute-start | bytes 196616 | tf_op jit(solution)/shard_map/small_weights/ppermute | solution.py:346
  11.9 1.3 collective-permute-start.4
  13.2 0.8 constant_dynamic-update-slice_fusion.7
  14.0 2.2 collective-permute-done.4
  16.2 0.7 constant_dynamic-update-slice_fusion.3
  17.0 0.7 copy-done.15
  17.7 0.9 constant_dynamic-slice_fusion.1
  18.9 0.9 constant_dynamic-slice_fusion
  19.9 1.6 collective-permute-start.15
  21.5 6.5 %collective-permute-done.15 = bf16[1024,128]{1,0:T(8,128)(2,1)S(1)} collective-permute-done((bf16[1024,128]{1,0:T(8,128)(2,1)S(1)}, bf16[1024,128]{1,0:T(8,128)(2,1)S(1)}, u32[]{:S(2)}, u32[]{:S(2)}) %collective-permute-start.15) | collective-permute-done | bytes 262176 | tf_op jit(solution)/shard_map/far_weights/ppermute | solution.py:365
  28.1 0.8 pad_maximum_fusion.2
  29.8 1.6 collective-permute-start.1
  31.3 1.7 collective-permute-start
  33.1 2.3 %constant_dynamic-slice_fusion.3 = bf16[256,2048]{1,0:T(8,128)(2,1)} fusion(bf16[512,2048]{1,0:T(8,128)(2,1)} %proj_ref.1, s32[]{:T(128)S(6)} %select_n.43), kind=kLoop, calls=%fused_computation.59 | loop fusion | bytes 2097156 | tf_op jit(solution)/shard_map/near_weights/dynamic_slice | solution.py:374
  35.4 2.4 %collective-permute-start.13 = (bf16[256,2048]{1,0:T(8,128)(2,1)}, bf16[256,2048]{1,0:T(8,128)(2,1)}, u32[]{:S(2)}, u32[]{:S(2)}) collective-permute-start(bf16[256,2048]{1,0:T(8,128)(2,1)} %constant_dynamic-slice_fusion.3), channel_id=1, source_target_pairs={{0,12},{4,0},{8,4},{12,8},{1,13},{5,1},{9,5},{13,9},{2,14},{6,2},{... | collective-permute-start | bytes 3145736 | tf_op jit(solution)/shard_map/near_weights/ppermute | solution.py:378
  37.8 1.3 copy.25
  39.0 6.0 %all-to-all-start.1 = ((bf16[16,16,16,128]{3,1,0,2:T(8,128)(2,1)}), bf16[16,16,16,128]{3,1,0,2:T(8,128)(2,1)S(1)}, u32[]{:S(2)}, u32[]{:S(2)}) async-start(bf16[16,16,16,128]{3,1,0,2:T(8,128)(2,1)} %bitcast.106), calls=%async_computation.1 | async-start | bytes 2097152 | tf_op jit(solution)/shard_map/all_to_all | solution.py:381
  45.0 2.3 %constant_dynamic-slice_fusion.4 = bf16[1024,512]{1,0:T(8,128)(2,1)} fusion(bf16[2048,512]{1,0:T(8,128)(2,1)} %fc_ref.1, s32[]{:T(128)S(6)} %select_n.42), kind=kLoop, calls=%fused_computation.60 | loop fusion | bytes 2097156 | tf_op jit(solution)/shard_map/near_weights/dynamic_slice | solution.py:373
  47.3 3.1 %collective-permute-start.11 = (bf16[1024,512]{1,0:T(8,128)(2,1)}, bf16[1024,512]{1,0:T(8,128)(2,1)}, u32[]{:S(2)}, u32[]{:S(2)}) collective-permute-start(bf16[1024,512]{1,0:T(8,128)(2,1)} %constant_dynamic-slice_fusion.4), channel_id=1, source_target_pairs={{0,12},{4,0},{8,4},{12,8},{1,13},{5,1},{9,5},{13,9},{2,14},{6,2},{... | collective-permute-start | bytes 3145736 | tf_op jit(solution)/shard_map/near_weights/ppermute | solution.py:378
  51.0 1.5 collective-permute-start.2
  52.6 9.3 %collective-permute-done.2.low_ref = bf16[64,2048]{1,0:T(8,128)(2,1)S(1)} collective-permute-done((bf16[64,2048]{1,0:T(8,128)(2,1)S(1)}, bf16[64,2048]{1,0:T(8,128)(2,1)S(1)}, u32[]{:S(2)}, u32[]{:S(2)}) %collective-permute-start.2) | collective-permute-done | bytes 262176 | tf_op jit(solution)/shard_map/gather_tokens/ppermute | solution.py:358
  61.8 1.0 collective-permute-start.3
  62.9 1.0 negate_select_fusion
  63.9 7.5 %collective-permute-done.13.proj_down_ref = bf16[256,2048]{1,0:T(8,128)(2,1)} collective-permute-done((bf16[256,2048]{1,0:T(8,128)(2,1)}, bf16[256,2048]{1,0:T(8,128)(2,1)}, u32[]{:S(2)}, u32[]{:S(2)}) %collective-permute-start.13) | collective-permute-done | bytes 1048608 | tf_op jit(solution)/shard_map/near_weights/ppermute | solution.py:378
  71.4 3.8 %collective-permute-done.9.proj_up_ref = bf16[256,2048]{1,0:T(8,128)(2,1)} collective-permute-done((bf16[256,2048]{1,0:T(8,128)(2,1)}, bf16[256,2048]{1,0:T(8,128)(2,1)}, u32[]{:S(2)}, u32[]{:S(2)}) %collective-permute-start.9) | collective-permute-done | bytes 1048608 | tf_op jit(solution)/shard_map/near_weights/ppermute | solution.py:378
  75.2 16.2 %collective-permute-done.11.fc_down_ref = bf16[1024,512]{1,0:T(8,128)(2,1)} collective-permute-done((bf16[1024,512]{1,0:T(8,128)(2,1)}, bf16[1024,512]{1,0:T(8,128)(2,1)}, u32[]{:S(2)}, u32[]{:S(2)}) %collective-permute-start.11) | collective-permute-done | bytes 1048608 | tf_op jit(solution)/shard_map/near_weights/ppermute | solution.py:378
  91.4 2.9 %collective-permute-done.7.fc_up_ref = bf16[1024,512]{1,0:T(8,128)(2,1)} collective-permute-done((bf16[1024,512]{1,0:T(8,128)(2,1)}, bf16[1024,512]{1,0:T(8,128)(2,1)}, u32[]{:S(2)}, u32[]{:S(2)}) %collective-permute-start.7) | collective-permute-done | bytes 1048608 | tf_op jit(solution)/shard_map/near_weights/ppermute | solution.py:378
  94.3 0.7 copy-done.7
  95.0 1.1 copy-done.1
  96.1 1.9 copy-done.4
  98.0 0.9 copy-done.6
  99.0 0.9 copy-done.8
  99.9 3.6 %qkv.1 = (bf16[512,2048]{1,0:T(8,128)(2,1)S(1)}, bf16[4,768,128]{2,1,0:T(8,128)(2,1)S(1)}) custom-call(s32[3]{0:T(128)S(1)} %pad_add_fusion.place_ref, bf16[128,2048]{1,0:T(8,128)(2,1)S(1)} %fusion.6.own_ref, bf16[128,2048]{1,0:T(8,128)(2,1)S(1)} %copy-done.1, bf16[64,2048]{1,0:T(8,128)(2,1)S(1)} %copy-done.6, bf16[64,2048]{1,0:T(8,128)(2,1)S(1)} %copy-done.8, ...), custom_call_target="tpu_custom_call" | custom-call | flops 1610612736 | bytes 4194304 | tf_op jit(solution)/shard_map/qkv/pallas_call | solution.py:303
  103.5 1.3 copy-done.10
  104.8 15.6 %all_to_all.25.sent_ref = bf16[4,768,128]{2,1,0:T(8,128)(2,1)S(1)} all-to-all(bf16[4,768,128]{2,1,0:T(8,128)(2,1)S(1)} %get-tuple-element.8), channel_id=1, replica_groups=mesh['z'=8,'core'=2,'y'=4,'x'=4] {'y'}, dimensions={0} | all-to-all | bytes 1572864 | tf_op jit(solution)/shard_map/all_to_all | solution.py:397
  120.4 36.9 %attend.1 = bf16[4,256,128]{2,1,0:T(8,128)(2,1)} custom-call(s32[8,128]{1,0:T(8,128)S(1)} %bitcast.105, s32[8]{0:T(128)S(1)} %bitcast.103, s32[8]{0:T(128)S(1)} %bitcast.102, bf16[4,768,128]{2,1,0:T(8,128)(2,1)S(1)} %all_to_all.25.sent_ref, bf16[256,16,128]{2,1,0:T(8,128)(2,1)S(1)} %bitcast.100), custom_call_target="tpu_custom_call" | custom-call | flops 2147483648 | bytes 4194304 | tf_op jit(solution)/shard_map/attend/pallas_call | solution.py:303
  157.3 3.4 %all-to-all-start.2 = ((bf16[4,256,128]{2,1,0:T(8,128)(2,1)}), bf16[4,256,128]{2,1,0:T(8,128)(2,1)S(1)}, u32[]{:S(2)}, u32[]{:S(2)}) async-start(bf16[4,256,128]{2,1,0:T(8,128)(2,1)} %attend.1), calls=%async_computation.2 | async-start | bytes 524288 | tf_op jit(solution)/shard_map/all_to_all | solution.py:413
  160.8 7.2 %all-to-all-done.2.heads_ref = bf16[4,256,128]{2,1,0:T(8,128)(2,1)S(1)} async-done(((bf16[4,256,128]{2,1,0:T(8,128)(2,1)}), bf16[4,256,128]{2,1,0:T(8,128)(2,1)S(1)}, u32[]{:S(2)}, u32[]{:S(2)}) %all-to-all-start.2) | async-done | bytes 262176 | tf_op jit(solution)/shard_map/all_to_all | solution.py:413
  167.9 21.3 %mix.1 = bf16[4,128,2048]{2,1,0:T(8,128)(2,1)} custom-call(s32[3]{0:T(128)S(1)} %pad_add_fusion.place_ref, bf16[512,2048]{1,0:T(8,128)(2,1)} %copy-done.10, bf16[2048,512]{1,0:T(8,128)(2,1)} %fc_ref.1, bf16[512,2048]{1,0:T(8,128)(2,1)} %proj_ref.1, bf16[1024,512]{1,0:T(8,128)(2,1)} %collective-permute-done.7.fc_up_ref, ...), custom_call_target="tpu_custom_call" | custom-call | flops 8589934592 | bytes 4194304 | tf_op jit(solution)/shard_map/mix/pallas_call | solution.py:303
  189.2 1.4 slice_bitcast_fusion.5
  191.2 3.0 %collective-permute-start.18 = (bf16[64,2048]{1,0:T(8,128)(2,1)S(1)}, bf16[64,2048]{1,0:T(8,128)(2,1)S(1)}, u32[]{:S(2)}, u32[]{:S(2)}) collective-permute-start(bf16[64,2048]{1,0:T(8,128)(2,1)S(1)} %get-tuple-element.12), channel_id=1, source_target_pairs={{0,3},{1,0},{2,1},{3,2},{4,7},{5,4},{6,5},{7,6},{8,11},{9,8},{10,9... | collective-permute-start | bytes 786440 | tf_op jit(solution)/shard_map/reduce_tokens/ppermute | solution.py:425
  194.2 5.1 %collective-permute-done.16 = bf16[64,2048]{1,0:T(8,128)(2,1)S(1)} collective-permute-done((bf16[64,2048]{1,0:T(8,128)(2,1)S(1)}, bf16[64,2048]{1,0:T(8,128)(2,1)S(1)}, u32[]{:S(2)}, u32[]{:S(2)}) %collective-permute-start.16) | collective-permute-done | bytes 262176 | tf_op jit(solution)/shard_map/reduce_tokens/ppermute | solution.py:424
  199.5 3.0 %collective-permute-start.19 = (bf16[128,2048]{1,0:T(8,128)(2,1)S(1)}, bf16[128,2048]{1,0:T(8,128)(2,1)S(1)}, u32[]{:S(2)}, u32[]{:S(2)}) collective-permute-start(bf16[128,2048]{1,0:T(8,128)(2,1)S(1)} %pad_maximum_fusion.1), channel_id=1, source_target_pairs={{0,3},{1,0},{2,1},{3,2},{4,7},{5,4},{6,5},{7,6},{8,11},{9,8},{10,9... | collective-permute-start | bytes 1572872 | tf_op jit(solution)/shard_map/reduce_tokens/ppermute | solution.py:433
  202.7 8.9 %collective-permute-done.19 = bf16[128,2048]{1,0:T(8,128)(2,1)S(1)} collective-permute-done((bf16[128,2048]{1,0:T(8,128)(2,1)S(1)}, bf16[128,2048]{1,0:T(8,128)(2,1)S(1)}, u32[]{:S(2)}, u32[]{:S(2)}) %collective-permute-start.19) | collective-permute-done | bytes 524320 | tf_op jit(solution)/shard_map/reduce_tokens/ppermute | solution.py:433
  211.6 3.5 %collective-permute-done.17 = bf16[128,2048]{1,0:T(8,128)(2,1)S(1)} collective-permute-done((bf16[128,2048]{1,0:T(8,128)(2,1)S(1)}, bf16[128,2048]{1,0:T(8,128)(2,1)S(1)}, u32[]{:S(2)}, u32[]{:S(2)}) %collective-permute-start.17) | collective-permute-done | bytes 524320 | tf_op jit(solution)/shard_map/reduce_tokens/ppermute | solution.py:432
  215.2 1.1 fusion.9
  (94 shorter events, 2.8 us)
Async XLA Ops:
  6.5 14.9 %copy-start.16 = (bf16[1,64,128]{2,1,0:T(8,128)(2,1)S(1)}, bf16[1,64,128]{2,1,0:T(8,128)(2,1)}, u32[]{:S(2)}) copy-start(bf16[1,64,128]{2,1,0:T(8,128)(2,1)} %param.13) | copy-start | bytes 49156
  6.5 22.3 %copy-start.17 = (bf16[2048]{0:T(1024)(128)(2,1)S(1)}, bf16[2048]{0:T(1024)(128)(2,1)}, u32[]{:S(2)}) copy-start(bf16[2048]{0:T(1024)(128)(2,1)} %param.11) | copy-start | bytes 12292
  6.5 22.3 %copy-start.11 = (bf16[1,128,2048]{2,1,0:T(8,128)(2,1)S(1)}, bf16[1,128,2048]{2,1,0:T(8,128)(2,1)}, u32[]{:S(2)}) copy-start(bf16[1,128,2048]{2,1,0:T(8,128)(2,1)} %param.10) | copy-start | bytes 1572868
  6.5 88.4 %all-gather.5.cloned.1.call-start = ((), (), s32[]{:S(2)}) async-start(), calls=%async_computation.3 | async-start | bytes 3342336 | tf_op jit(solution)/shard_map/small_weights/all_gather | solution.py:352
  7.4 8.8 %collective-permute-start.6 = (bf16[256,128]{1,0:T(8,128)(2,1)S(1)}, bf16[256,128]{1,0:T(8,128)(2,1)S(1)}, u32[]{:S(2)}, u32[]{:S(2)}) collective-permute-start(bf16[256,128]{1,0:T(8,128)(2,1)S(1)} %pad_maximum_fusion.4), channel_id=1, source_target_pairs={{0,4},{4,8},{8,12},{12,0},{1,5},{5,9},{9,13},{13,1},{2,6},{6,10},{... | collective-permute-start | bytes 196616 | tf_op jit(solution)/shard_map/small_weights/ppermute | solution.py:347
  9.0 7.2 %collective-permute-start.5 = (bf16[256,128]{1,0:T(8,128)(2,1)S(1)}, bf16[256,128]{1,0:T(8,128)(2,1)S(1)}, u32[]{:S(2)}, u32[]{:S(2)}) collective-permute-start(bf16[256,128]{1,0:T(8,128)(2,1)S(1)} %pad_maximum_fusion.4), channel_id=1, source_target_pairs={{0,8},{4,12},{8,0},{12,4},{1,9},{5,13},{9,1},{13,5},{2,10},{6,14},... | collective-permute-start | bytes 196616 | tf_op jit(solution)/shard_map/small_weights/ppermute | solution.py:346
  11.9 4.3 %collective-permute-start.4 = (bf16[256,128]{1,0:T(8,128)(2,1)S(1)}, bf16[256,128]{1,0:T(8,128)(2,1)S(1)}, u32[]{:S(2)}, u32[]{:S(2)}) collective-permute-start(bf16[256,128]{1,0:T(8,128)(2,1)S(1)} %pad_maximum_fusion.4), channel_id=1, source_target_pairs={{0,12},{4,0},{8,4},{12,8},{1,13},{5,1},{9,5},{13,9},{2,14},{6,2},{... | collective-permute-start | bytes 196616 | tf_op jit(solution)/shard_map/small_weights/ppermute | solution.py:345
  17.0 0.7 copy-start.15
  17.7 150.2 %all-gather.7.cloned.1.call-start = ((), (), s32[]{:S(2)}) async-start(), calls=%async_computation.4 | async-start | bytes 5570560 | tf_op jit(solution)/shard_map/far_weights/all_gather | solution.py:368
  19.9 8.2 %collective-permute-start.15 = (bf16[1024,128]{1,0:T(8,128)(2,1)S(1)}, bf16[1024,128]{1,0:T(8,128)(2,1)S(1)}, u32[]{:S(2)}, u32[]{:S(2)}) collective-permute-start(bf16[1024,128]{1,0:T(8,128)(2,1)S(1)} %pad_maximum_fusion.3), channel_id=1, source_target_pairs={{0,8},{4,12},{8,0},{12,4},{1,9},{5,13},{9,1},{13,5},{2,10},{6,14},... | collective-permute-start | bytes 786440 | tf_op jit(solution)/shard_map/far_weights/ppermute | solution.py:365
  28.9 8.9 %copy-start.14 = (bf16[1,16,16,16,128]{4,3,2,1,0:T(8,128)(2,1)S(1)}, bf16[1,16,16,16,128]{4,3,2,1,0:T(8,128)(2,1)}, u32[]{:S(2)}) copy-start(bf16[1,16,16,16,128]{4,3,2,1,0:T(8,128)(2,1)} %param.16) | copy-start | bytes 3145732
  29.8 21.0 %collective-permute-start.1 = (bf16[128,2048]{1,0:T(8,128)(2,1)S(1)}, bf16[128,2048]{1,0:T(8,128)(2,1)S(1)}, u32[]{:S(2)}, u32[]{:S(2)}) collective-permute-start(bf16[128,2048]{1,0:T(8,128)(2,1)S(1)} %fusion.6.own_ref), channel_id=1, source_target_pairs={{0,1},{1,2},{2,3},{3,0},{4,5},{5,6},{6,7},{7,4},{8,9},{9,10},{10,1... | collective-permute-start | bytes 1572872 | tf_op jit(solution)/shard_map/gather_tokens/ppermute | solution.py:356
  31.3 19.6 %collective-permute-start = (bf16[128,2048]{1,0:T(8,128)(2,1)S(1)}, bf16[128,2048]{1,0:T(8,128)(2,1)S(1)}, u32[]{:S(2)}, u32[]{:S(2)}) collective-permute-start(bf16[128,2048]{1,0:T(8,128)(2,1)S(1)} %fusion.6.own_ref), channel_id=1, source_target_pairs={{0,3},{1,0},{2,1},{3,2},{4,7},{5,4},{6,5},{7,6},{8,11},{9,8},{10,9... | collective-permute-start | bytes 1572872 | tf_op jit(solution)/shard_map/gather_tokens/ppermute | solution.py:357
  35.4 36.0 %collective-permute-start.13 = (bf16[256,2048]{1,0:T(8,128)(2,1)}, bf16[256,2048]{1,0:T(8,128)(2,1)}, u32[]{:S(2)}, u32[]{:S(2)}) collective-permute-start(bf16[256,2048]{1,0:T(8,128)(2,1)} %constant_dynamic-slice_fusion.3), channel_id=1, source_target_pairs={{0,12},{4,0},{8,4},{12,8},{1,13},{5,1},{9,5},{13,9},{2,14},{6,2},{... | collective-permute-start | bytes 3145736 | tf_op jit(solution)/shard_map/near_weights/ppermute | solution.py:378
  37.8 37.5 %collective-permute-start.9 = (bf16[256,2048]{1,0:T(8,128)(2,1)}, bf16[256,2048]{1,0:T(8,128)(2,1)}, u32[]{:S(2)}, u32[]{:S(2)}) collective-permute-start(bf16[256,2048]{1,0:T(8,128)(2,1)} %constant_dynamic-slice_fusion.3), channel_id=1, source_target_pairs={{0,4},{4,8},{8,12},{12,0},{1,5},{5,9},{9,13},{13,1},{2,6},{6,10},{... | collective-permute-start | bytes 3145736 | tf_op jit(solution)/shard_map/near_weights/ppermute | solution.py:378
  39.0 11.4 %copy-start.2 = (s32[1,8]{1,0:T(1,128)S(1)}, s32[1,8]{1,0:T(1,128)}, u32[]{:S(2)}) copy-start(s32[1,8]{1,0:T(1,128)} %param.19) | copy-start | bytes 100
  39.0 11.6 %copy-start.3 = (s32[1,8]{1,0:T(1,128)S(1)}, s32[1,8]{1,0:T(1,128)}, u32[]{:S(2)}) copy-start(s32[1,8]{1,0:T(1,128)} %param.18) | copy-start | bytes 100
  39.0 65.8 %all-to-all-start.1 = ((bf16[16,16,16,128]{3,1,0,2:T(8,128)(2,1)}), bf16[16,16,16,128]{3,1,0,2:T(8,128)(2,1)S(1)}, u32[]{:S(2)}, u32[]{:S(2)}) async-start(bf16[16,16,16,128]{3,1,0,2:T(8,128)(2,1)} %bitcast.106), calls=%async_computation.1 | async-start | bytes 2097152 | tf_op jit(solution)/shard_map/all_to_all | solution.py:381
  47.3 44.1 %collective-permute-start.11 = (bf16[1024,512]{1,0:T(8,128)(2,1)}, bf16[1024,512]{1,0:T(8,128)(2,1)}, u32[]{:S(2)}, u32[]{:S(2)}) collective-permute-start(bf16[1024,512]{1,0:T(8,128)(2,1)} %constant_dynamic-slice_fusion.4), channel_id=1, source_target_pairs={{0,12},{4,0},{8,4},{12,8},{1,13},{5,1},{9,5},{13,9},{2,14},{6,2},{... | collective-permute-start | bytes 3145736 | tf_op jit(solution)/shard_map/near_weights/ppermute | solution.py:378
  50.7 43.6 %collective-permute-start.7 = (bf16[1024,512]{1,0:T(8,128)(2,1)}, bf16[1024,512]{1,0:T(8,128)(2,1)}, u32[]{:S(2)}, u32[]{:S(2)}) collective-permute-start(bf16[1024,512]{1,0:T(8,128)(2,1)} %constant_dynamic-slice_fusion.4), channel_id=1, source_target_pairs={{0,4},{4,8},{8,12},{12,0},{1,5},{5,9},{9,13},{13,1},{2,6},{6,10},{... | collective-permute-start | bytes 3145736 | tf_op jit(solution)/shard_map/near_weights/ppermute | solution.py:378
  51.0 11.9 %copy-start = (bf16[128,2048]{1,0:T(8,128)(2,1)}, bf16[128,2048]{1,0:T(8,128)(2,1)S(1)}, u32[]{:S(2)}) copy-start(bf16[128,2048]{1,0:T(8,128)(2,1)S(1)} %collective-permute-done.right_ref) | copy-start | bytes 1572868
  51.0 10.8 %collective-permute-start.2 = (bf16[64,2048]{1,0:T(8,128)(2,1)S(1)}, bf16[64,2048]{1,0:T(8,128)(2,1)S(1)}, u32[]{:S(2)}, u32[]{:S(2)}) collective-permute-start(bf16[64,2048]{1,0:T(8,128)(2,1)S(1)} %slice.80), channel_id=1, source_target_pairs={{0,1},{1,2},{2,3},{3,0},{4,5},{5,6},{6,7},{7,4},{8,9},{9,10},{10,1... | collective-permute-start | bytes 786440 | tf_op jit(solution)/shard_map/gather_tokens/ppermute | solution.py:358
  61.8 33.2 %copy-start.5 = (bf16[64,2048]{1,0:T(8,128)(2,1)}, bf16[64,2048]{1,0:T(8,128)(2,1)S(1)}, u32[]{:S(2)}) copy-start(bf16[64,2048]{1,0:T(8,128)(2,1)S(1)} %collective-permute-done.2.low_ref) | copy-start | bytes 786436
  61.8 32.5 %collective-permute-start.3 = (bf16[64,2048]{1,0:T(8,128)(2,1)S(1)}, bf16[64,2048]{1,0:T(8,128)(2,1)S(1)}, u32[]{:S(2)}, u32[]{:S(2)}) collective-permute-start(bf16[64,2048]{1,0:T(8,128)(2,1)S(1)} %slice.81), channel_id=1, source_target_pairs={{0,3},{1,0},{2,1},{3,2},{4,7},{5,4},{6,5},{7,6},{8,11},{9,8},{10,9... | collective-permute-start | bytes 786440 | tf_op jit(solution)/shard_map/gather_tokens/ppermute | solution.py:359
  71.4 89.3 %collective-permute-start.14 = (bf16[256,2048]{1,0:T(8,128)(2,1)}, bf16[256,2048]{1,0:T(8,128)(2,1)}, u32[]{:S(2)}, u32[]{:S(2)}) collective-permute-start(bf16[256,2048]{1,0:T(8,128)(2,1)} %collective-permute-done.13.proj_down_ref), channel_id=1, source_target_pairs={{0,16},{16,0},{1,17},{17,1},{2,18},{18,2},{3,19},{19,3},{4,20},{20... | collective-permute-start | bytes 3145736 | tf_op jit(solution)/shard_map/near_weights/ppermute | solution.py:379
  75.2 85.5 %collective-permute-start.10 = (bf16[256,2048]{1,0:T(8,128)(2,1)}, bf16[256,2048]{1,0:T(8,128)(2,1)}, u32[]{:S(2)}, u32[]{:S(2)}) collective-permute-start(bf16[256,2048]{1,0:T(8,128)(2,1)} %collective-permute-done.9.proj_up_ref), channel_id=1, source_target_pairs={{0,16},{16,0},{1,17},{17,1},{2,18},{18,2},{3,19},{19,3},{4,20},{20... | collective-permute-start | bytes 3145736 | tf_op jit(solution)/shard_map/near_weights/ppermute | solution.py:379
  91.4 69.3 %collective-permute-start.12 = (bf16[1024,512]{1,0:T(8,128)(2,1)}, bf16[1024,512]{1,0:T(8,128)(2,1)}, u32[]{:S(2)}, u32[]{:S(2)}) collective-permute-start(bf16[1024,512]{1,0:T(8,128)(2,1)} %collective-permute-done.11.fc_down_ref), channel_id=1, source_target_pairs={{0,16},{16,0},{1,17},{17,1},{2,18},{18,2},{3,19},{19,3},{4,20},{20... | collective-permute-start | bytes 3145736 | tf_op jit(solution)/shard_map/near_weights/ppermute | solution.py:379
  94.3 66.5 %collective-permute-start.8 = (bf16[1024,512]{1,0:T(8,128)(2,1)}, bf16[1024,512]{1,0:T(8,128)(2,1)}, u32[]{:S(2)}, u32[]{:S(2)}) collective-permute-start(bf16[1024,512]{1,0:T(8,128)(2,1)} %collective-permute-done.7.fc_up_ref), channel_id=1, source_target_pairs={{0,16},{16,0},{1,17},{17,1},{2,18},{18,2},{3,19},{19,3},{4,20},{20... | collective-permute-start | bytes 3145736 | tf_op jit(solution)/shard_map/near_weights/ppermute | solution.py:379
  94.3 0.7 copy-start.7
  95.0 1.1 copy-start.1
  96.1 1.9 copy-start.4
  98.0 0.9 copy-start.6
  99.0 0.9 copy-start.8
  99.9 20.5 %copy-start.9 = (s32[1,8,128]{2,1,0:T(8,128)S(1)}, s32[1,8,128]{2,1,0:T(8,128)}, u32[]{:S(2)}) copy-start(s32[1,8,128]{2,1,0:T(8,128)} %param.17) | copy-start | bytes 12292
  103.5 1.3 copy-start.10
  157.3 10.6 %all-to-all-start.2 = ((bf16[4,256,128]{2,1,0:T(8,128)(2,1)}), bf16[4,256,128]{2,1,0:T(8,128)(2,1)S(1)}, u32[]{:S(2)}, u32[]{:S(2)}) async-start(bf16[4,256,128]{2,1,0:T(8,128)(2,1)} %attend.1), calls=%async_computation.2 | async-start | bytes 524288 | tf_op jit(solution)/shard_map/all_to_all | solution.py:413
  189.2 10.1 %copy-start.13 = (bf16[4,128,2048]{2,1,0:T(8,128)(2,1)S(1)}, bf16[4,128,2048]{2,1,0:T(8,128)(2,1)}, u32[]{:S(2)}) copy-start(bf16[4,128,2048]{2,1,0:T(8,128)(2,1)} %mix.1) | copy-start | bytes 6291460
  190.7 24.5 %copy-start.12 = (bf16[1,128,2048]{2,1,0:T(8,128)(2,1)S(1)}, bf16[1,128,2048]{2,1,0:T(8,128)(2,1)}, u32[]{:S(2)}) copy-start(bf16[1,128,2048]{2,1,0:T(8,128)(2,1)} %param.10) | copy-start | bytes 1572868
  190.7 8.7 %collective-permute-start.16 = (bf16[64,2048]{1,0:T(8,128)(2,1)S(1)}, bf16[64,2048]{1,0:T(8,128)(2,1)S(1)}, u32[]{:S(2)}, u32[]{:S(2)}) collective-permute-start(bf16[64,2048]{1,0:T(8,128)(2,1)S(1)} %get-tuple-element.11), channel_id=1, source_target_pairs={{0,1},{1,2},{2,3},{3,0},{4,5},{5,6},{6,7},{7,4},{8,9},{9,10},{10,1... | collective-permute-start | bytes 786440 | tf_op jit(solution)/shard_map/reduce_tokens/ppermute | solution.py:424
  191.2 8.1 %collective-permute-start.18 = (bf16[64,2048]{1,0:T(8,128)(2,1)S(1)}, bf16[64,2048]{1,0:T(8,128)(2,1)S(1)}, u32[]{:S(2)}, u32[]{:S(2)}) collective-permute-start(bf16[64,2048]{1,0:T(8,128)(2,1)S(1)} %get-tuple-element.12), channel_id=1, source_target_pairs={{0,3},{1,0},{2,1},{3,2},{4,7},{5,4},{6,5},{7,6},{8,11},{9,8},{10,9... | collective-permute-start | bytes 786440 | tf_op jit(solution)/shard_map/reduce_tokens/ppermute | solution.py:425
  199.5 12.1 %collective-permute-start.19 = (bf16[128,2048]{1,0:T(8,128)(2,1)S(1)}, bf16[128,2048]{1,0:T(8,128)(2,1)S(1)}, u32[]{:S(2)}, u32[]{:S(2)}) collective-permute-start(bf16[128,2048]{1,0:T(8,128)(2,1)S(1)} %pad_maximum_fusion.1), channel_id=1, source_target_pairs={{0,3},{1,0},{2,1},{3,2},{4,7},{5,4},{6,5},{7,6},{8,11},{9,8},{10,9... | collective-permute-start | bytes 1572872 | tf_op jit(solution)/shard_map/reduce_tokens/ppermute | solution.py:433
  202.6 12.6 %collective-permute-start.17 = (bf16[128,2048]{1,0:T(8,128)(2,1)S(1)}, bf16[128,2048]{1,0:T(8,128)(2,1)S(1)}, u32[]{:S(2)}, u32[]{:S(2)}) collective-permute-start(bf16[128,2048]{1,0:T(8,128)(2,1)S(1)} %pad_maximum_fusion), channel_id=1, source_target_pairs={{0,1},{1,2},{2,3},{3,0},{4,5},{5,6},{6,7},{7,4},{8,9},{9,10},{10,1... | collective-permute-start | bytes 1572872 | tf_op jit(solution)/shard_map/reduce_tokens/ppermute | solution.py:432
Sparse Core Ops, SparseCore 0:
  17.8 39.7 all-gather.4
  59.4 41.5 all-gather.6

commit v3 on v2

v3 whole, which is shorter than its diff:
```python
import functools

import jax
import jax.numpy as jnp
from jax import lax
from jax.experimental import pallas as pl
from jax.experimental.pallas import tpu as pltpu
from jax.sharding import Mesh
from jax.sharding import PartitionSpec as P

ROT = 32
LOG2E = 1.4426950408889634
MIB = 1024 * 1024
epsilon = 1e-05


def layer_norm(rows, gain):
    values = rows.astype(jnp.float32)
    centred = values - jnp.mean(values, axis=-1, keepdims=True)
    variance = jnp.mean(centred * centred, axis=-1, keepdims=True)
    return (centred * lax.rsqrt(variance + epsilon) * gain.astype(jnp.float32)).astype(jnp.bfloat16)


def rotation_tables(request_lengths, counts, first_token, tokens, block_len, lanes):
    half = ROT // 2
    ends = jnp.cumsum(request_lengths)
    starts = ends - request_lengths
    index = first_token + jnp.arange(tokens, dtype=jnp.int32)
    inside = (index[:, None] >= starts[None, :]) & (index[:, None] < ends[None, :])
    position = (
        jnp.sum(jnp.where(inside, (counts * block_len - starts)[None, :], 0), axis=-1) + index
    )
    frequency = 10000.0 ** (-2.0 * jnp.arange(half, dtype=jnp.float32) / ROT)
    lane = jnp.arange(lanes, dtype=jnp.int32)
    spread = jnp.where(lane < ROT, jnp.tile(frequency, lanes // half), 0.0)
    angle = position.astype(jnp.float32)[:, None] * spread[None, :]
    sine = jnp.sin(angle)
    return jnp.cos(angle), jnp.where(lane[None, :] < half, -sine, sine)


def qkv_kernel(
    ring, place_ref, cosine_ref, sine_ref, own_ref, right_ref, opposite_ref, left_ref,
    gathered_ref, rows_ref, *refs
):
    sent_refs, (weight_ref, cos_ref, sin_ref, sems) = refs[:ring], refs[ring:]
    x = place_ref[0]
    part = own_ref.shape[0]
    tokens, lanes = cos_ref.shape
    head = lanes // 2

    copies = [
        pltpu.make_async_copy(source, target, sems.at[k])
        for k, (source, target) in enumerate(
            ((gathered_ref, weight_ref), (cosine_ref, cos_ref), (sine_ref, sin_ref))
        )
    ]
    for step, piece in enumerate((own_ref, right_ref, opposite_ref, left_ref)):
        begin = pl.multiple_of(lax.rem(x + step, ring) * part, part)
        target = rows_ref.at[pl.ds(begin, part), :]
        copies.append(pltpu.make_async_copy(piece, target, sems.at[len(copies)]))
    for copy in copies:
        copy.start()
    for copy in copies:
        copy.wait()
    lane = lax.broadcasted_iota(jnp.int32, (tokens, lanes), 1)

    def rotated(field):
        other = jnp.where(
            lane < ROT // 2, pltpu.roll(field, lanes - ROT // 2, 1), pltpu.roll(field, ROT // 2, 1)
        )
        return field * cos_ref[...] + other * sin_ref[...]

    def product(begin, size):
        weight = jnp.concatenate(
            [weight_ref[g, begin : begin + size, :] for g in range(weight_ref.shape[0])], axis=1
        )
        return lax.dot_general(
            rows_ref[...], weight, (((1,), (1,)), ((), ())), preferred_element_type=jnp.float32
        )

    for pair in range(ring // 2):
        both = product(pair * 2 * lanes, 2 * lanes)
        for k in range(2):
            field = rotated(both[:, k * lanes : (k + 1) * lanes])
            sent_refs[2 * pair + k][:tokens, :] = field.astype(jnp.bfloat16)
    queries = product(ring * lanes, ring * head)
    for d in range(ring):
        field = queries[:, d // 2 * lanes : (d // 2 + 1) * lanes]
        if d % 2:
            field = pltpu.roll(field, head, 1)
        field = rotated(field)
        top, bottom = field[: tokens // 2], pltpu.roll(field[tokens // 2 :], head, 1)
        folded = jnp.where(lane[: tokens // 2] < head, top, bottom)
        sent_refs[d][tokens:, :] = folded.astype(jnp.bfloat16)


def attention_kernel(
    chunk, tile, scale, ring, place_ref, table_ref, count_ref, length_ref, pool_ref, *refs
):
    sent_refs, out_refs = refs[:ring], refs[ring : 2 * ring]
    query_ref, fresh_ref, worth_ref, result_ref, key_ref, value_ref, score_ref = refs[2 * ring :]
    y = place_ref[1]
    tokens, lanes = query_ref.shape
    head = lanes // 2
    part = tokens // ring
    block_len = pool_ref.shape[1]
    requests = table_ref.shape[0]
    per_chunk = chunk // block_len
    factor = scale * LOG2E
    unroll = 8
    block_lane = lax.broadcasted_iota(jnp.int32, (block_len, lanes), 1)
    fold_lane = lax.broadcasted_iota(jnp.int32, (part // 2, lanes), 1)
    part_lane = lax.broadcasted_iota(jnp.int32, (part, lanes), 1)
    one = jnp.ones((), jnp.bfloat16)
    nil = jnp.zeros((), jnp.bfloat16)

    fresh_ref[tokens:, :] = jnp.zeros((fresh_ref.shape[0] - tokens, lanes), jnp.bfloat16)
    worth_ref[tokens:, :] = jnp.zeros((fresh_ref.shape[0] - tokens, lanes), jnp.bfloat16)
    for i in range(ring):
        both = sent_refs[i][:part, :]
        origin = lax.rem(y + ring - i, ring) * part
        block = pl.ds(pl.multiple_of(origin, part), part)
        fresh_ref[block, :] = both
        worth_ref[block, :] = jnp.where(part_lane < head, one, both)
        folded = sent_refs[i][part:, :].astype(jnp.float32)
        for k in range(2):
            unfolded = folded if k == 0 else pltpu.roll(folded, head, 1)
            begin = pl.multiple_of(origin + k * (part // 2), part // 2)
            query_ref[pl.ds(begin, part // 2), :] = jnp.where(
                fold_lane < head, unfolded, 0.0
            ).astype(jnp.bfloat16)

    def dot_t(a, b):
        return lax.dot_general(a, b, (((1,), (1,)), ((), ())), preferred_element_type=jnp.float32)

    def peak(highest, scores):
        for k in range(chunk // lanes):
            highest = jnp.maximum(highest, scores[:, k * lanes : (k + 1) * lanes])
        return highest

    def request(r, start):
        length = length_ref[r]
        count = count_ref[r]
        chunks = (count + per_chunk - 1) // per_chunk

        def gather(i, _):
            for u in range(unroll):
                b = i * unroll + u
                block = pool_ref[table_ref[r, jnp.minimum(b, count - 1)]]
                where = pl.ds(pl.multiple_of(b * block_len, block_len), block_len)
                key_ref[where, :] = block
                paired = jnp.where(block_lane < head, one, block)
                value_ref[where, :] = jnp.where(b < count, paired, nil)
            return 0

        lax.fori_loop(0, chunks * (per_chunk // unroll), gather, 0)
        first = start // 16 * 16
        tiles = (start + length - first + tile - 1) // tile

        def one_tile(i, _):
            row = pl.multiple_of(jnp.minimum(first + i * tile, tokens - tile), 16)
            rows = pl.ds(row, tile)
            query = query_ref[rows, :]
            fresh_chunks = (row + tile - first + chunk - 1) // chunk
            own = row + lax.broadcasted_iota(jnp.int32, (tile, chunk), 0)
            column = first + lax.broadcasted_iota(jnp.int32, (tile, chunk), 1)

            def at(j):
                return pl.ds(pl.multiple_of(j * chunk, chunk), chunk)

            def fresh_at(j):
                return pl.ds(pl.multiple_of(first + j * chunk, 16), chunk)

            def look(j, highest):
                scores = dot_t(query, key_ref[at(j), :])
                score_ref[:, at(j)] = scores
                return peak(highest, scores)

            def look_fresh(j, highest):
                scores = dot_t(query, fresh_ref[fresh_at(j), :])
                other = column + j * chunk
                visible = (other >= start) & (other <= own)
                scores = jnp.where(visible, scores, -1e30)
                score_ref[:, at(chunks + j)] = scores
                return peak(highest, scores)

            highest = jnp.full((tile, lanes), -1e30, jnp.float32)
            highest = lax.fori_loop(0, chunks, look, highest)
            highest = lax.fori_loop(0, fresh_chunks, look_fresh, highest)
            top = factor * jnp.max(highest, axis=-1, keepdims=True)

            def weigh(j, acc):
                weights = jnp.exp2(factor * score_ref[:, at(j)] - top).astype(jnp.bfloat16)
                return acc + jnp.dot(
                    weights, value_ref[at(j), :], preferred_element_type=jnp.float32
                )

            def weigh_fresh(j, acc):
                weights = jnp.exp2(factor * score_ref[:, at(chunks + j)] - top).astype(jnp.bfloat16)
                return acc + jnp.dot(
                    weights, worth_ref[fresh_at(j), :], preferred_element_type=jnp.float32
                )

            acc = jnp.zeros((tile, lanes), jnp.float32)
            acc = lax.fori_loop(0, chunks, weigh, acc)
            acc = lax.fori_loop(0, fresh_chunks, weigh_fresh, acc)
            result = (acc / pltpu.roll(acc, head, 1)).astype(jnp.bfloat16)
            place = row + lax.broadcasted_iota(jnp.int32, (tile, lanes), 0)
            inside = (place >= start) & (place < start + length)
            result_ref[rows, :] = jnp.where(inside, result, result_ref[rows, :])
            return 0

        lax.fori_loop(0, tiles, one_tile, 0)
        return start + length

    lax.fori_loop(0, requests, request, 0)
    for i in range(ring):
        begin = pl.multiple_of(lax.rem(y + i, ring) * part, part)
        top = result_ref[pl.ds(begin, part // 2), :].astype(jnp.float32)
        bottom = result_ref[pl.ds(begin + part // 2, part // 2), :].astype(jnp.float32)
        out_refs[i][...] = jnp.where(fold_lane < head, pltpu.roll(top, head, 1), bottom).astype(
            jnp.bfloat16
        )


def gelu(value):
    return jax.nn.gelu(value, approximate=True).astype(jnp.bfloat16)


def dot(a, b):
    return jnp.dot(a, b, preferred_element_type=jnp.float32)


def hide_kernel(rows_ref, *refs):
    half = len(refs) // 2
    for fc_ref, hidden_ref in zip(refs[:half], refs[half:]):
        hidden_ref[...] = gelu(dot(rows_ref[...], fc_ref[...]))


def mix_kernel(
    steps, hide, place_ref, own_ref, near_ref, other_ref,
    head0_ref, head1_ref, head2_ref, head3_ref,
    given_ref, proj_own_hbm, proj_near_hbm, proj_other_hbm, gathered_ref, *refs
):
    out_refs, refs = refs[:-7], refs[-7:]
    attention_ref, held_ref, far_ref, proj_own_ref, proj_near_ref, proj_other_ref, sems = refs
    x = place_ref[0]
    tokens, units = own_ref.shape
    width = proj_own_ref.shape[1]
    groups, held, lanes = gathered_ref.shape
    begin = held - 2 * units
    head = lanes // 2
    ring = attention_ref.shape[1] // head
    part = tokens // ring
    stripe = 512

    moves = [(given_ref, far_ref)]
    for rows in [pl.ds(begin, units)] * hide + [pl.ds(held - units, units), pl.ds(0, begin)]:
        moves.append((gathered_ref.at[:, rows, :], held_ref.at[:, rows, :]))
    moves += [
        (proj_own_hbm, proj_own_ref), (proj_near_hbm, proj_near_ref),
        (proj_other_hbm, proj_other_ref),
    ]
    copies = [
        pltpu.make_async_copy(source, target, sems.at[k])
        for k, (source, target) in enumerate(moves)
    ]
    for copy in copies:
        copy.start()
    fold_lane = lax.broadcasted_iota(jnp.int32, (tokens // 2, lanes), 1)
    for k, (first, second) in enumerate(((head0_ref, head1_ref), (head2_ref, head3_ref))):
        a, b = first[...].astype(jnp.float32), second[...].astype(jnp.float32)
        columns = slice(k * lanes, (k + 1) * lanes)
        attention_ref[: tokens // 2, columns] = jnp.where(
            fold_lane < head, a, pltpu.roll(b, head, 1)
        ).astype(jnp.bfloat16)
        attention_ref[tokens // 2 :, columns] = jnp.where(
            fold_lane < head, pltpu.roll(a, head, 1), b
        ).astype(jnp.bfloat16)

    def take(ref):
        return jnp.concatenate(
            [
                ref[pl.ds(pl.multiple_of(lax.rem(x + step, ring) * part, part), part), :]
                for step in steps
            ],
            axis=0,
        )

    if hide:
        for copy in copies[:2]:
            copy.wait()
        fc = jnp.concatenate(
            [
                jnp.concatenate(
                    [
                        held_ref[g, begin + b * lanes : begin + (b + 1) * lanes, :]
                        for b in range(units // lanes)
                    ],
                    axis=1,
                )
                for g in range(groups)
            ],
            axis=0,
        )
        out_refs[-1][...] = gelu(dot(far_ref[...], fc))
        far_ref, out_refs = out_refs[-1], out_refs[:-1]
    for copy in copies[2 * hide :]:
        copy.wait()
    values = [take(ref) for ref in (own_ref, near_ref, other_ref, far_ref, attention_ref)]
    per = stripe // lanes
    for i in range(width // stripe):
        columns = slice(i * stripe, (i + 1) * stripe)
        weights = [ref[:, columns] for ref in (proj_own_ref, proj_near_ref, proj_other_ref)]
        for rows in (slice(held - units, held), slice(0, ring * head)):
            weights.append(
                jnp.concatenate([held_ref[i * per + g, rows, :] for g in range(per)], axis=1)
            )
        total = dot(values[0], weights[0])
        for value, weight in zip(values[1:], weights[1:]):
            total += dot(value, weight)
        total = total.astype(jnp.bfloat16)
        row = 0
        for out_ref in out_refs:
            size = out_ref.shape[0]
            out_ref[:, columns] = total[row : row + size]
            row += size


def call(kernel, name, out_shape, smem, vmem, operands, scratch, limit, flops, anywhere=0):
    specs = [pl.BlockSpec(memory_space=pltpu.SMEM)] * smem
    specs += [pl.BlockSpec(memory_space=pltpu.VMEM)] * vmem
    specs += [pl.BlockSpec(memory_space=pltpu.HBM)] * anywhere
    several = isinstance(out_shape, (tuple, list))
    spec = pl.BlockSpec(memory_space=pltpu.VMEM)
    return pl.pallas_call(
        kernel,
        out_shape=out_shape,
        in_specs=specs,
        out_specs=[spec] * len(out_shape) if several else spec,
        scratch_shapes=scratch,
        compiler_params=pltpu.CompilerParams(vmem_limit_bytes=limit * MIB),
        cost_estimate=pl.CostEstimate(flops=flops, bytes_accessed=4 * MIB, transcendentals=0),
        name=name,
    )(*operands)


def per_device(
    tokens, ln_gain, w_qkv, w_out, w_fc, w_proj, pool_kv, block_table, block_count, lengths
):
    bf16 = jnp.bfloat16
    ring = lax.axis_size("x")
    groups = lax.axis_size("z") * lax.axis_size("core")
    x, y = lax.axis_index("x"), lax.axis_index("y")
    core = lax.axis_index("core")
    group = lax.axis_index("z") * lax.axis_size("core") + core
    place = jnp.stack([x, y, core]).astype(jnp.int32)
    up = [(i, (i + 1) % ring) for i in range(ring)]
    down = [(i, (i - 1) % ring) for i in range(ring)]
    across = [(i, (i + 2) % ring) for i in range(ring)]
    swap = [(0, 1), (1, 0)]

    own = tokens[0]
    part, width = own.shape
    row_tok = part * ring
    group_tok = row_tok * ring
    local_pool = pool_kv[0]
    blk_dev, block_len, _, lanes = local_pool.shape
    pool_blocks = blk_dev * ring * ring
    head = lanes // 2
    units = w_fc.shape[1]
    slab = width // groups

    with jax.named_scope("small_weights"):
        small = jnp.concatenate([w_qkv[:, 0, :].T, w_out[0]], axis=0)
        slices = [
            small,
            lax.ppermute(small, "y", down),
            lax.ppermute(small, "y", across),
            lax.ppermute(small, "y", up),
        ]
        packed = jnp.concatenate(
            [s[head : 3 * head] for s in slices] + [s[:head] for s in slices], axis=0
        )
        qkv_weight = lax.all_gather(packed, ("z", "core"), axis=0, tiled=False)

    normed = layer_norm(own, ln_gain)
    fan = [(i, (i + 1) % ring) for i in range(ring)]
    fan += [(ring + i, ring + (i - 1) % ring) for i in range(ring)]
    with jax.named_scope("gather_tokens"):
        left = lax.ppermute(normed, "x", up)
        right = lax.ppermute(normed, "x", down)
        opposite = lax.ppermute(jnp.where(core == 0, left, right), ("core", "x"), fan)

    def after(value, other):
        return lax.optimization_barrier((value, other))[0]

    with jax.named_scope("far_weights"):
        fc_slab = lax.dynamic_slice_in_dim(after(w_fc, normed), group * slab, slab, 0)
        pieces = [fc_slab[:, b : b + lanes] for b in range(0, units, lanes)]
        proj_slab = lax.dynamic_slice_in_dim(after(w_proj, normed), group * slab, slab, 1)
        payload = jnp.concatenate(pieces + [proj_slab], axis=0)
        far = lax.ppermute(payload, "y", across)

    with jax.named_scope("near_weights"):
        fc_near = lax.ppermute(after(w_fc, payload), ("core", "y"), fan)

    pooled = lax.all_to_all(
        after(local_pool, left), ("y", "x"), split_axis=2, concat_axis=0, tiled=True
    )
    pooled = pooled.reshape(pool_blocks, block_len, lanes)
    cosine, sine = rotation_tables(
        lengths[0], block_count[0], y * row_tok, row_tok, block_len, lanes
    )
    payload = row_tok + row_tok // 2
    sent_shape = jax.ShapeDtypeStruct((payload, lanes), bf16)
    rows, *sent = call(
        functools.partial(qkv_kernel, ring), "qkv",
        [jax.ShapeDtypeStruct((row_tok, width), bf16)] + [sent_shape] * ring,
        1, 0, (place, cosine, sine, normed, right, opposite, left, qkv_weight),
        [
            pltpu.VMEM((groups, 3 * head * ring, lanes), bf16),
            pltpu.VMEM((row_tok, lanes), jnp.float32),
            pltpu.VMEM((row_tok, lanes), jnp.float32),
            pltpu.SemaphoreType.DMA((7,)),
        ],
        56, 3_000 * MIB, 7,
    )
    gathered = lax.all_gather(
        after(jnp.concatenate([s[3 * head :] for s in slices] + [far], axis=0), (rows, pooled, fc_near)),
        ("z", "core"), axis=0, tiled=False,
    )
    ways = (None, up, across, down)

    def exchange(pieces):
        return [pieces[0]] + [lax.ppermute(p, "y", w) for p, w in zip(pieces[1:], ways[1:])]

    received = exchange(sent)
    work = 2 * row_tok * width * units
    hidden_shape = jax.ShapeDtypeStruct((row_tok, units), bf16)
    work = 2 * row_tok * width * units
    fc_other = lax.ppermute(fc_near, "core", swap)
    own_hidden, near_hidden = call(
        hide_kernel, "hide", [hidden_shape] * 2, 0, 3, (rows, w_fc, fc_near), (), 8, 2 * work
    )
    (other_hidden,) = call(
        hide_kernel, "hide", [hidden_shape], 0, 2, (rows, fc_other), (), 8, work
    )
    proj_near = lax.ppermute(after(w_proj, tuple(received[1:])), ("core", "y"), fan)

    keys = block_table.shape[2] * block_len
    chunk, tile = 512, 256
    most = -(-(group_tok // 4 + tile + 16) // chunk) * chunk
    heads = call(
        functools.partial(attention_kernel, chunk, tile, head**-0.5, ring), "attend",
        [jax.ShapeDtypeStruct((row_tok // 2, lanes), bf16)] * ring,
        4, 1 + ring, (after(place, (own_hidden, near_hidden, other_hidden)), block_table[0], block_count[0], lengths[0], pooled, *received),
        [
            pltpu.VMEM((group_tok, lanes), bf16),
            pltpu.VMEM((group_tok + most, lanes), bf16),
            pltpu.VMEM((group_tok + most, lanes), bf16),
            pltpu.VMEM((group_tok, lanes), bf16),
            pltpu.VMEM((keys, lanes), bf16),
            pltpu.VMEM((keys, lanes), bf16),
            pltpu.VMEM((tile, keys + most), jnp.float32),
        ],
        12, 30_000 * MIB,
    )
    proj_other = lax.ppermute(after(proj_near, heads[0]), "core", swap)
    heads = exchange(heads)
    block_shape = jax.ShapeDtypeStruct((part, width), bf16)

    def mix(steps, shapes, given, hide):
        return call(
            functools.partial(mix_kernel, steps, hide), "mix", shapes, 1, 7,
            (
                place, own_hidden, near_hidden, other_hidden,
                heads[0], heads[3], heads[2], heads[1],
                given, w_proj, proj_near, proj_other, gathered,
            ),
            [
                pltpu.VMEM((row_tok, ring * head), bf16),
                pltpu.VMEM(gathered.shape, bf16),
                pltpu.VMEM(given.shape, bf16),
                pltpu.VMEM(w_proj.shape, bf16),
                pltpu.VMEM(w_proj.shape, bf16),
                pltpu.VMEM(w_proj.shape, bf16),
                pltpu.SemaphoreType.DMA((7,)),
            ],
            52, (len(steps) + 2 * hide) * work, 5,
        )

    out2, far_hidden = mix((2,), [block_shape, hidden_shape], rows, True)
    out1, out3, out0 = mix((1, 3, 0), [block_shape] * 3, far_hidden, False)

    with jax.named_scope("reduce_tokens"):
        passed = lax.ppermute(out2, ("core", "x"), fan).astype(jnp.float32)

        def joined(block, which):
            added = jnp.where(core == which, passed, 0.0)
            return (block.astype(jnp.float32) + added).astype(bf16)

        a = lax.ppermute(joined(out1, 0), "x", up).astype(jnp.float32)
        b = lax.ppermute(joined(out3, 1), "x", down).astype(jnp.float32)
    summed = out0.astype(jnp.float32) + a + b
    return (own.astype(jnp.float32) + summed).astype(bf16)[None]


def solution(mesh):
    grid = Mesh(mesh.devices.reshape(8, 2, 4, 4), ("z", "core", "y", "x"))
    grp, pool = ("z", "core"), ("y", "x")
    in_specs = (
        P(grp, pool, None),
        P(),
        P(grp, pool, None),
        P(pool, None, grp),
        P(None, pool),
        P(pool, None),
        P(grp, pool, None, None, None),
        P(grp, None, None),
        P(grp, None),
        P(grp, None),
    )
    return jax.shard_map(
        per_device, mesh=grid, in_specs=in_specs, out_specs=P(grp, pool, None), check_vma=False
    )
```

time: 226 us -> 182 us (0.81); the launches traced: 223 us -> 182 us
  waiting for transfers between devices: 73.1 us -> 45.2 us
  blocking collectives: 15.6 us -> 0 us
  Pallas kernels: 61.8 us -> 70 us
  starting transfers between devices: 34.9 us -> 27.6 us
  other arithmetic: 5.2 us -> 8.8 us
  local copies, waits for them, and re-layouts: 18.8 us -> 16.4 us
    ppermute x15, waiting for transfers between devices: 63.8 us -> 32.4 us  [the longest x1 12.2 us: per_device(): b = lax.ppermute(joined(out3, 1), 'x', down).astype(jnp.float32)]
    all_to_all x1 -> x0, blocking collectives: 15.6 us -> none  [per_device(): lax.all_to_all(sent, 'y', split_axis=0, concat_axis=0, tiled=True)]
    pallas_call x3 -> x6, Pallas kernels: 61.8 us -> 70 us  [call(): pl.pallas_call(kernel, out_shape=out_shape, in_specs=specs, out_specs=[sp...]
    dynamic_slice x5 -> x0, local copies, waits for them, and re-layouts: 6.47 us -> none  [the longest x1 2.33 us: per_device(): lax.dynamic_slice_in_dim(w_proj, core * (units // 2), units // 2, 0)]
    all_to_all x2 -> x1, starting transfers between devices: 9.4 us -> 4.22 us  [per_device(): lax.all_to_all(after(local_pool, left), ('y', 'x'), split_axis=2, concat_...]
    unnamed x52, local copies, waits for them, and re-layouts: 10.6 us -> 13.8 us
    ppermute x1, waiting for transfers between devices: 0.01 us -> 3.01 us  [per_device(): left = lax.ppermute(normed, 'x', up)]
    ppermute x1, waiting for transfers between devices: 0.01 us -> 2.71 us  [per_device(): lax.ppermute(small, 'y', across)]
  transfers between devices with their start and end apart: 24 -> 23, of which waited for: 11 -> 11; matrix products, arithmetic and copies ran while one was open for 5% -> 10% of each run, Pallas kernels for 18% -> 34%
where the time goes in v3:
time: 182 us
  Pallas kernels  70 us (38%)
  waiting for transfers between devices  45.2 us (25%)
  starting transfers between devices  27.6 us (15%)
  local copies, waits for them, and re-layouts  16.4 us (9%)
  between operations  13.7 us (8%)
  other arithmetic  8.8 us (5%)
    pallas_call x6, Pallas kernels, call(): pl.pallas_call(kernel, out_shape=out_shape, in_specs=specs, out_specs=[sp...  70 us
    unnamed x52, local copies, waits for them, and re-layouts  13.8 us
    ppermute x1, waiting for transfers between devices, per_device(): b = lax.ppermute(joined(out3, 1), 'x', down).astype(jnp.float32)  12.2 us
    ppermute x1, waiting for transfers between devices, per_device(): lax.ppermute(jnp.where(core == 0, left, right), ('core', 'x'), fan)  11.8 us
    ppermute x6, starting transfers between devices, exchange(): lax.ppermute(p, 'y', w)  8.94 us
    all_to_all x1, waiting for transfers between devices, per_device(): lax.all_to_all(after(local_pool, left), ('y', 'x'), split_axis=2, concat_...  6.4 us
    ppermute x6, waiting for transfers between devices, exchange(): lax.ppermute(p, 'y', w)  5.5 us
    all_to_all x1, starting transfers between devices, per_device(): lax.all_to_all(after(local_pool, left), ('y', 'x'), split_axis=2, concat_...  4.22 us
  transfers between devices with their start and end apart: 23, of which 11 were waited for; matrix products, arithmetic and copies ran while one was open for 10% of the time, Pallas kernels for 34%

profile of v3, /device:TPU:160, one launch (start us, length us, event | category | flops | bytes accessed | tf_op | source)
XLA Modules:
  0.0 181.7 jit_solution(7852048072324249819)
XLA Ops:
  6.6 0.9 pad_maximum_fusion
  7.5 3.0 %collective-permute-start.3 = (bf16[256,128]{1,0:T(8,128)(2,1)S(1)}, bf16[256,128]{1,0:T(8,128)(2,1)S(1)}, u32[]{:S(2)}, u32[]{:S(2)}) collective-permute-start(bf16[256,128]{1,0:T(8,128)(2,1)S(1)} %pad_maximum_fusion), channel_id=1, source_target_pairs={{0,12},{4,0},{8,4},{12,8},{1,13},{5,1},{9,5},{13,9},{2,14},{6,2},{... | collective-permute-start | bytes 196616 | tf_op jit(solution)/shard_map/small_weights/ppermute | solution.py:378
  11.2 1.0 collective-permute-start.5
  12.1 0.8 constant_dynamic-update-slice_fusion.7
  12.9 0.7 constant_dynamic-update-slice_fusion.16
  13.6 2.7 %collective-permute-done.4 = bf16[256,128]{1,0:T(8,128)(2,1)S(1)} collective-permute-done((bf16[256,128]{1,0:T(8,128)(2,1)S(1)}, bf16[256,128]{1,0:T(8,128)(2,1)S(1)}, u32[]{:S(2)}, u32[]{:S(2)}) %collective-permute-start.4) | collective-permute-done | bytes 65568 | tf_op jit(solution)/shard_map/small_weights/ppermute | solution.py:379
  17.0 0.7 constant_dynamic-update-slice_fusion.3
  17.8 0.7 copy-done.18
  18.5 0.7 convert_element_type.50
  19.2 1.2 convert_reduce_fusion
  20.4 1.3 fusion.4
  22.1 2.8 %collective-permute-start = (bf16[128,2048]{1,0:T(8,128)(2,1)S(1)}, bf16[128,2048]{1,0:T(8,128)(2,1)S(1)}, u32[]{:S(2)}, u32[]{:S(2)}) collective-permute-start(bf16[128,2048]{1,0:T(8,128)(2,1)S(1)} %fusion.6.own_ref), channel_id=1, source_target_pairs={{0,3},{1,0},{2,1},{3,2},{4,7},{5,4},{6,5},{7,6},{8,11},{9,8},{10,9... | collective-permute-start | bytes 1572872 | tf_op jit(solution)/shard_map/gather_tokens/ppermute | solution.py:392
  25.0 1.4 constant_dynamic-update-slice_fusion.11
  26.4 1.4 constant_dynamic-update-slice_fusion.10
  27.7 1.4 constant_dynamic-update-slice_fusion.9
  29.1 1.4 constant_dynamic-update-slice_fusion.8
  30.5 1.6 dynamic-slice_dynamic-update-slice_fusion
  32.0 1.3 collective-permute-start.16
  33.8 1.3 copy.15
  35.1 3.0 %collective-permute-done.1.left_ref = bf16[128,2048]{1,0:T(8,128)(2,1)S(1)} collective-permute-done((bf16[128,2048]{1,0:T(8,128)(2,1)S(1)}, bf16[128,2048]{1,0:T(8,128)(2,1)S(1)}, u32[]{:S(2)}, u32[]{:S(2)}) %collective-permute-start.1) | collective-permute-done | bytes 524320 | tf_op jit(solution)/shard_map/gather_tokens/ppermute | solution.py:391
  38.1 4.2 %all-to-all-start = ((bf16[16,16,16,128]{3,1,0,2:T(8,128)(2,1)}), bf16[16,16,16,128]{3,1,0,2:T(8,128)(2,1)S(1)}, u32[]{:S(2)}, u32[]{:S(2)}) async-start(bf16[16,16,16,128]{3,1,0,2:T(8,128)(2,1)} %bitcast.54), calls=%async_computation | async-start | bytes 2097152 | tf_op jit(solution)/shard_map/all_to_all | solution.py:408
  42.5 2.0 %collective-permute-start.2 = (bf16[128,2048]{1,0:T(8,128)(2,1)S(1)}, bf16[128,2048]{1,0:T(8,128)(2,1)}, u32[]{:S(2)}, u32[]{:S(2)}) collective-permute-start(bf16[128,2048]{1,0:T(8,128)(2,1)S(1)} %broadcast_select_fusion), channel_id=1, source_target_pairs={{0,1},{1,2},{2,3},{3,0},{16,19},{17,16},{18,17},{19,18},{4,5},{5,6... | collective-permute-start | bytes 1572872 | tf_op jit(solution)/shard_map/gather_tokens/ppermute | solution.py:393
  45.2 1.8 %negate_select_fusion = (f32[512,128]{1,0:T(8,128)}, f32[512,128]{1,0:T(8,128)}) fusion(f32[128]{0:T(128)S(1)} %compare_select_fusion, f32[512]{0:T(512)S(1)} %add_convert_fusion, pred[128]{0:T(512)(128)(4,1)S(1)} %iota_compare_fusion), kind=kLoop, calls=%fused_computation.19 | loop fusion | flops 196608 | bytes 526976 | tf_op jit(solution)/shard_map/jit(_where)/select_n | solution.py:38
  47.0 1.0 constant_dynamic-update-slice_fusion.12
  48.0 11.8 %collective-permute-done.2.opposite_ref = bf16[128,2048]{1,0:T(8,128)(2,1)} collective-permute-done((bf16[128,2048]{1,0:T(8,128)(2,1)S(1)}, bf16[128,2048]{1,0:T(8,128)(2,1)}, u32[]{:S(2)}, u32[]{:S(2)}) %collective-permute-start.2) | collective-permute-done | bytes 524320 | tf_op jit(solution)/shard_map/gather_tokens/ppermute | solution.py:393
  59.8 7.6 %qkv.1 = (bf16[512,2048]{1,0:T(8,128)(2,1)}, bf16[768,128]{1,0:T(8,128)(2,1)}, bf16[768,128]{1,0:T(8,128)(2,1)}, bf16[768,128]{1,0:T(8,128)(2,1)}, bf16[768,128]{1,0:T(8,128)(2,1)}) custom-call(s32[3]{0:T(128)} %pad_add_fusion.place_ref, f32[512,128]{1,0:T(8,128)} %get-tuple-element.62.cosine_ref, f32[512,128]{1,0:T(8,128)} %get-tuple-element.61.sine_ref, ...), custom_call_target="tpu_custom_call" | custom-call | flops 3145728000 | bytes 4194304 | tf_op jit(solution)/shard_map/qkv/pallas_call | solution.py:336
  67.5 6.4 %all-to-all-done = bf16[16,16,16,128]{3,1,0,2:T(8,128)(2,1)S(1)} async-done(((bf16[16,16,16,128]{3,1,0,2:T(8,128)(2,1)}), bf16[16,16,16,128]{3,1,0,2:T(8,128)(2,1)S(1)}, u32[]{:S(2)}, u32[]{:S(2)}) %all-to-all-start) | async-done | bytes 1048608 | tf_op jit(solution)/shard_map/all_to_all | solution.py:408
  74.1 2.0 %collective-permute-start.9 = (bf16[768,128]{1,0:T(8,128)(2,1)}, bf16[768,128]{1,0:T(8,128)(2,1)S(1)}, u32[]{:S(2)}, u32[]{:S(2)}) collective-permute-start(bf16[768,128]{1,0:T(8,128)(2,1)} %get-tuple-element.39), channel_id=1, source_target_pairs={{0,8},{4,12},{8,0},{12,4},{1,9},{5,13},{9,1},{13,5},{2,10},{6,14},... | collective-permute-start | bytes 589832 | tf_op jit(solution)/shard_map/ppermute | solution.py:436
  76.1 2.4 %collective-permute-start.10 = (bf16[768,128]{1,0:T(8,128)(2,1)}, bf16[768,128]{1,0:T(8,128)(2,1)S(1)}, u32[]{:S(2)}, u32[]{:S(2)}) collective-permute-start(bf16[768,128]{1,0:T(8,128)(2,1)} %get-tuple-element.40), channel_id=1, source_target_pairs={{0,12},{4,0},{8,4},{12,8},{1,13},{5,1},{9,5},{13,9},{2,14},{6,2},{... | collective-permute-start | bytes 589832 | tf_op jit(solution)/shard_map/ppermute | solution.py:436
  78.4 1.6 copy-done
  80.0 1.4 hide.3.other_ref
  81.5 0.8 copy-done.1
  82.3 5.1 %hide.2 = (bf16[512,512]{1,0:T(8,128)(2,1)S(1)}, bf16[512,512]{1,0:T(8,128)(2,1)S(1)}) custom-call(bf16[512,2048]{1,0:T(8,128)(2,1)S(1)} %copy-done, bf16[2048,512]{1,0:T(8,128)(2,1)} %refs_0_.1, bf16[2048,512]{1,0:T(8,128)(2,1)} %collective-permute-done.6.refs_1_), custom_call_target="tpu_custom_call" | custom-call | flops 2147483648 | bytes 4194304 | tf_op jit(solution)/shard_map/hide/pallas_call | solution.py:336
  87.4 0.8 copy-done.3
  88.6 38.9 %attend.1 = (bf16[256,128]{1,0:T(8,128)(2,1)S(1)}, bf16[256,128]{1,0:T(8,128)(2,1)S(1)}, bf16[256,128]{1,0:T(8,128)(2,1)S(1)}, bf16[256,128]{1,0:T(8,128)(2,1)S(1)}) custom-call(s32[3]{0:T(128)S(1)} %copy-done.5, s32[8,128]{1,0:T(8,128)S(1)} %bitcast.59, s32[8]{0:T(128)S(1)} %bitcast.58, s32[8]{0:T(128)S(1)} %bitcast.57, bf16[256,16,128]{2,1,0:T(8,128)(2,1)S(1)} %bitcast.55, ...), custom_call_target="tpu_custom_call" | custom-call | flops 31457280000 | bytes 4194304 | tf_op jit(solution)/shard_map/attend/pallas_call | solution.py:336
  127.6 3.0 %collective-permute-start.11 = (bf16[256,128]{1,0:T(8,128)(2,1)S(1)}, bf16[256,128]{1,0:T(8,128)(2,1)S(1)}, u32[]{:S(2)}, u32[]{:S(2)}) collective-permute-start(bf16[256,128]{1,0:T(8,128)(2,1)S(1)} %get-tuple-element.42), channel_id=1, source_target_pairs={{0,12},{4,0},{8,4},{12,8},{1,13},{5,1},{9,5},{13,9},{2,14},{6,2},{... | collective-permute-start | bytes 196616 | tf_op jit(solution)/shard_map/ppermute | solution.py:436
  131.2 1.0 collective-permute-start.13
  132.2 1.8 %collective-permute-done.11.head1_ref = bf16[256,128]{1,0:T(8,128)(2,1)S(1)} collective-permute-done((bf16[256,128]{1,0:T(8,128)(2,1)S(1)}, bf16[256,128]{1,0:T(8,128)(2,1)S(1)}, u32[]{:S(2)}, u32[]{:S(2)}) %collective-permute-start.11) | collective-permute-done | bytes 65568 | tf_op jit(solution)/shard_map/ppermute | solution.py:436
  134.0 3.0 %collective-permute-done.12.head2_ref = bf16[256,128]{1,0:T(8,128)(2,1)S(1)} collective-permute-done((bf16[256,128]{1,0:T(8,128)(2,1)S(1)}, bf16[256,128]{1,0:T(8,128)(2,1)S(1)}, u32[]{:S(2)}, u32[]{:S(2)}) %collective-permute-start.12) | collective-permute-done | bytes 65568 | tf_op jit(solution)/shard_map/ppermute | solution.py:436
  137.0 0.7 collective-permute-done.13.head3_ref
  137.7 7.7 %mix.2 = (bf16[128,2048]{1,0:T(8,128)(2,1)S(1)}, bf16[512,512]{1,0:T(8,128)(2,1)S(1)}) custom-call(s32[3]{0:T(128)S(1)} %copy-done.5, bf16[512,512]{1,0:T(8,128)(2,1)S(1)} %get-tuple-element.33.own_ref, bf16[512,512]{1,0:T(8,128)(2,1)} %copy-done.3, bf16[512,512]{1,0:T(8,128)(2,1)} %copy-done.1, bf16[256,128]{1,0:T(8,128)(2,1)S(1)} %get-tuple-element.41.head0_ref, ...), custom_call_target="tpu_custom_call" | custom-call | flops 3221225472 | bytes 4194304 | tf_op jit(solution)/shard_map/mix/pallas_call | solution.py:336
  145.4 0.8 copy-done.4
  146.2 0.7 collective-permute-start.17
  146.9 9.2 %mix.3 = (bf16[128,2048]{1,0:T(8,128)(2,1)S(1)}, bf16[128,2048]{1,0:T(8,128)(2,1)S(1)}, bf16[128,2048]{1,0:T(8,128)(2,1)S(1)}) custom-call(s32[3]{0:T(128)S(1)} %copy-done.5, bf16[512,512]{1,0:T(8,128)(2,1)} %copy-done.2, bf16[512,512]{1,0:T(8,128)(2,1)} %copy-done.3, bf16[512,512]{1,0:T(8,128)(2,1)} %copy-done.1, ...), custom_call_target="tpu_custom_call" | custom-call | flops 3221225472 | bytes 4194304 | tf_op jit(solution)/shard_map/mix/pallas_call | solution.py:336
  157.0 2.2 %collective-permute-start.19 = (bf16[128,2048]{1,0:T(8,128)(2,1)S(1)}, bf16[128,2048]{1,0:T(8,128)(2,1)S(1)}, u32[]{:S(2)}, u32[]{:S(2)}) collective-permute-start(bf16[128,2048]{1,0:T(8,128)(2,1)S(1)} %get-tuple-element.54), channel_id=1, source_target_pairs={{0,3},{1,0},{2,1},{3,2},{4,7},{5,4},{6,5},{7,6},{8,11},{9,8},{10,9... | collective-permute-start | bytes 1572872 | tf_op jit(solution)/shard_map/reduce_tokens/ppermute | solution.py:504
  159.1 12.2 %collective-permute-done.19 = bf16[128,2048]{1,0:T(8,128)(2,1)S(1)} collective-permute-done((bf16[128,2048]{1,0:T(8,128)(2,1)S(1)}, bf16[128,2048]{1,0:T(8,128)(2,1)S(1)}, u32[]{:S(2)}, u32[]{:S(2)}) %collective-permute-start.19) | collective-permute-done | bytes 524320 | tf_op jit(solution)/shard_map/reduce_tokens/ppermute | solution.py:504
  171.3 2.4 %collective-permute-done.18 = bf16[128,2048]{1,0:T(8,128)(2,1)S(1)} collective-permute-done((bf16[128,2048]{1,0:T(8,128)(2,1)S(1)}, bf16[128,2048]{1,0:T(8,128)(2,1)S(1)}, u32[]{:S(2)}, u32[]{:S(2)}) %collective-permute-start.18) | collective-permute-done | bytes 524320 | tf_op jit(solution)/shard_map/reduce_tokens/ppermute | solution.py:503
  173.7 1.1 fusion.12
  (82 shorter events, 5.2 us)
Async XLA Ops:
  6.5 15.2 %copy-start.11 = (bf16[1,128,2048]{2,1,0:T(8,128)(2,1)S(1)}, bf16[1,128,2048]{2,1,0:T(8,128)(2,1)}, u32[]{:S(2)}) copy-start(bf16[1,128,2048]{2,1,0:T(8,128)(2,1)} %param.10) | copy-start | bytes 1572868
  6.5 26.9 %copy-start.6 = (s32[1,8]{1,0:T(1,128)S(1)}, s32[1,8]{1,0:T(1,128)}, u32[]{:S(2)}) copy-start(s32[1,8]{1,0:T(1,128)} %param.19) | copy-start | bytes 100
  6.5 27.1 %copy-start.7 = (s32[1,8]{1,0:T(1,128)S(1)}, s32[1,8]{1,0:T(1,128)}, u32[]{:S(2)}) copy-start(s32[1,8]{1,0:T(1,128)} %param.18) | copy-start | bytes 100
  6.5 27.2 %copy-start.13 = (bf16[1,16,16,16,128]{4,3,2,1,0:T(8,128)(2,1)S(1)}, bf16[1,16,16,16,128]{4,3,2,1,0:T(8,128)(2,1)}, u32[]{:S(2)}) copy-start(bf16[1,16,16,16,128]{4,3,2,1,0:T(8,128)(2,1)} %param.16) | copy-start | bytes 3145732
  6.5 53.3 %all-gather.5.cloned.1.call-start = ((), (), s32[]{:S(2)}) async-start(), calls=%async_computation.1 | async-start | bytes 3342336 | tf_op jit(solution)/shard_map/small_weights/all_gather | solution.py:385
  7.5 6.1 %collective-permute-start.3 = (bf16[256,128]{1,0:T(8,128)(2,1)S(1)}, bf16[256,128]{1,0:T(8,128)(2,1)S(1)}, u32[]{:S(2)}, u32[]{:S(2)}) collective-permute-start(bf16[256,128]{1,0:T(8,128)(2,1)S(1)} %pad_maximum_fusion), channel_id=1, source_target_pairs={{0,12},{4,0},{8,4},{12,8},{1,13},{5,1},{9,5},{13,9},{2,14},{6,2},{... | collective-permute-start | bytes 196616 | tf_op jit(solution)/shard_map/small_weights/ppermute | solution.py:378
  10.5 5.8 %collective-permute-start.4 = (bf16[256,128]{1,0:T(8,128)(2,1)S(1)}, bf16[256,128]{1,0:T(8,128)(2,1)S(1)}, u32[]{:S(2)}, u32[]{:S(2)}) collective-permute-start(bf16[256,128]{1,0:T(8,128)(2,1)S(1)} %pad_maximum_fusion), channel_id=1, source_target_pairs={{0,8},{4,12},{8,0},{12,4},{1,9},{5,13},{9,1},{13,5},{2,10},{6,14},... | collective-permute-start | bytes 196616 | tf_op jit(solution)/shard_map/small_weights/ppermute | solution.py:379
  11.2 5.8 %collective-permute-start.5 = (bf16[256,128]{1,0:T(8,128)(2,1)S(1)}, bf16[256,128]{1,0:T(8,128)(2,1)S(1)}, u32[]{:S(2)}, u32[]{:S(2)}) collective-permute-start(bf16[256,128]{1,0:T(8,128)(2,1)S(1)} %pad_maximum_fusion), channel_id=1, source_target_pairs={{0,4},{4,8},{8,12},{12,0},{1,5},{5,9},{9,13},{13,1},{2,6},{6,10},{... | collective-permute-start | bytes 196616 | tf_op jit(solution)/shard_map/small_weights/ppermute | solution.py:380
  17.8 0.7 copy-start.18
  22.1 16.0 %copy-start.14 = (bf16[128,2048]{1,0:T(8,128)(2,1)}, bf16[128,2048]{1,0:T(8,128)(2,1)S(1)}, u32[]{:S(2)}) copy-start(bf16[128,2048]{1,0:T(8,128)(2,1)S(1)} %fusion.6.own_ref) | copy-start | bytes 1572868
  22.1 20.3 %collective-permute-start = (bf16[128,2048]{1,0:T(8,128)(2,1)S(1)}, bf16[128,2048]{1,0:T(8,128)(2,1)S(1)}, u32[]{:S(2)}, u32[]{:S(2)}) collective-permute-start(bf16[128,2048]{1,0:T(8,128)(2,1)S(1)} %fusion.6.own_ref), channel_id=1, source_target_pairs={{0,3},{1,0},{2,1},{3,2},{4,7},{5,4},{6,5},{7,6},{8,11},{9,8},{10,9... | collective-permute-start | bytes 1572872 | tf_op jit(solution)/shard_map/gather_tokens/ppermute | solution.py:392
  25.0 13.2 %collective-permute-start.1 = (bf16[128,2048]{1,0:T(8,128)(2,1)S(1)}, bf16[128,2048]{1,0:T(8,128)(2,1)S(1)}, u32[]{:S(2)}, u32[]{:S(2)}) collective-permute-start(bf16[128,2048]{1,0:T(8,128)(2,1)S(1)} %fusion.6.own_ref), channel_id=1, source_target_pairs={{0,1},{1,2},{2,3},{3,0},{4,5},{5,6},{6,7},{7,4},{8,9},{9,10},{10,1... | collective-permute-start | bytes 1572872 | tf_op jit(solution)/shard_map/gather_tokens/ppermute | solution.py:391
  32.0 15.0 %collective-permute-start.16 = (bf16[1024,128]{1,0:T(8,128)(2,1)}, bf16[1024,128]{1,0:T(8,128)(2,1)}, u32[]{:S(2)}, u32[]{:S(2)}) collective-permute-start(bf16[1024,128]{1,0:T(8,128)(2,1)} %dynamic-slice_dynamic-update-slice_fusion), channel_id=1, source_target_pairs={{0,8},{4,12},{8,0},{12,4},{1,9},{5,13},{9,1},{13,5},{2,10},{6,14},... | collective-permute-start | bytes 786440 | tf_op jit(solution)/shard_map/far_weights/ppermute | solution.py:403
  33.4 40.5 %collective-permute-start.6 = (bf16[2048,512]{1,0:T(8,128)(2,1)}, bf16[2048,512]{1,0:T(8,128)(2,1)}, u32[]{:S(2)}, u32[]{:S(2)}) collective-permute-start(bf16[2048,512]{1,0:T(8,128)(2,1)} %refs_0_.1), channel_id=1, source_target_pairs={{0,4},{4,8},{8,12},{12,0},{16,28},{20,16},{24,20},{28,24},{1,5},{5... | collective-permute-start | bytes 6291464 | tf_op jit(solution)/shard_map/near_weights/ppermute | solution.py:406
  38.1 8.8 %copy-start.16 = (bf16[128,2048]{1,0:T(8,128)(2,1)}, bf16[128,2048]{1,0:T(8,128)(2,1)S(1)}, u32[]{:S(2)}) copy-start(bf16[128,2048]{1,0:T(8,128)(2,1)S(1)} %collective-permute-done.1.left_ref) | copy-start | bytes 1572868
  38.1 35.7 %all-to-all-start = ((bf16[16,16,16,128]{3,1,0,2:T(8,128)(2,1)}), bf16[16,16,16,128]{3,1,0,2:T(8,128)(2,1)S(1)}, u32[]{:S(2)}, u32[]{:S(2)}) async-start(bf16[16,16,16,128]{3,1,0,2:T(8,128)(2,1)} %bitcast.54), calls=%async_computation | async-start | bytes 2097152 | tf_op jit(solution)/shard_map/all_to_all | solution.py:408
  42.4 95.3 %all-gather.7.cloned.1.call-start = ((), (), s32[]{:S(2)}) async-start(), calls=%async_computation.2 | async-start | bytes 5570560 | tf_op jit(solution)/shard_map/all_gather | solution.py:429
  42.4 17.4 %copy-start.15 = (bf16[128,2048]{1,0:T(8,128)(2,1)}, bf16[128,2048]{1,0:T(8,128)(2,1)S(1)}, u32[]{:S(2)}) copy-start(bf16[128,2048]{1,0:T(8,128)(2,1)S(1)} %collective-permute-done.right_ref) | copy-start | bytes 1572868
  42.5 17.3 %collective-permute-start.2 = (bf16[128,2048]{1,0:T(8,128)(2,1)S(1)}, bf16[128,2048]{1,0:T(8,128)(2,1)}, u32[]{:S(2)}, u32[]{:S(2)}) collective-permute-start(bf16[128,2048]{1,0:T(8,128)(2,1)S(1)} %broadcast_select_fusion), channel_id=1, source_target_pairs={{0,1},{1,2},{2,3},{3,0},{16,19},{17,16},{18,17},{19,18},{4,5},{5,6... | collective-permute-start | bytes 1572872 | tf_op jit(solution)/shard_map/gather_tokens/ppermute | solution.py:393
  48.0 19.5 %copy-start.17 = (bf16[1280,128]{1,0:T(8,128)(2,1)}, bf16[1280,128]{1,0:T(8,128)(2,1)S(1)}, u32[]{:S(2)}) copy-start(bf16[1280,128]{1,0:T(8,128)(2,1)S(1)} %constant_dynamic-update-slice_fusion.12) | copy-start | bytes 983044
  73.9 4.5 %collective-permute-start.7 = (bf16[2048,512]{1,0:T(8,128)(2,1)}, bf16[2048,512]{1,0:T(8,128)(2,1)S(1)}, u32[]{:S(2)}, u32[]{:S(2)}) collective-permute-start(bf16[2048,512]{1,0:T(8,128)(2,1)} %collective-permute-done.6.refs_1_), channel_id=1, source_target_pairs={{0,16},{16,0},{1,17},{17,1},{2,18},{18,2},{3,19},{19,3},{4,20},{20... | collective-permute-start | bytes 6291464 | tf_op jit(solution)/shard_map/ppermute | solution.py:442
  74.0 14.2 %collective-permute-start.8 = (bf16[768,128]{1,0:T(8,128)(2,1)}, bf16[768,128]{1,0:T(8,128)(2,1)S(1)}, u32[]{:S(2)}, u32[]{:S(2)}) collective-permute-start(bf16[768,128]{1,0:T(8,128)(2,1)} %get-tuple-element.38), channel_id=1, source_target_pairs={{0,4},{4,8},{8,12},{12,0},{1,5},{5,9},{9,13},{13,1},{2,6},{6,10},{... | collective-permute-start | bytes 589832 | tf_op jit(solution)/shard_map/ppermute | solution.py:436
  74.1 14.1 %collective-permute-start.9 = (bf16[768,128]{1,0:T(8,128)(2,1)}, bf16[768,128]{1,0:T(8,128)(2,1)S(1)}, u32[]{:S(2)}, u32[]{:S(2)}) collective-permute-start(bf16[768,128]{1,0:T(8,128)(2,1)} %get-tuple-element.39), channel_id=1, source_target_pairs={{0,8},{4,12},{8,0},{12,4},{1,9},{5,13},{9,1},{13,5},{2,10},{6,14},... | collective-permute-start | bytes 589832 | tf_op jit(solution)/shard_map/ppermute | solution.py:436
  76.1 12.1 %collective-permute-start.10 = (bf16[768,128]{1,0:T(8,128)(2,1)}, bf16[768,128]{1,0:T(8,128)(2,1)S(1)}, u32[]{:S(2)}, u32[]{:S(2)}) collective-permute-start(bf16[768,128]{1,0:T(8,128)(2,1)} %get-tuple-element.40), channel_id=1, source_target_pairs={{0,12},{4,0},{8,4},{12,8},{1,13},{5,1},{9,5},{13,9},{2,14},{6,2},{... | collective-permute-start | bytes 589832 | tf_op jit(solution)/shard_map/ppermute | solution.py:436
  78.4 1.6 copy-start
  81.5 0.8 copy-start.1
  82.3 5.9 %copy-start.10 = (bf16[512,2048]{1,0:T(8,128)(2,1)S(1)}, bf16[512,2048]{1,0:T(8,128)(2,1)}, u32[]{:S(2)}) copy-start(bf16[512,2048]{1,0:T(8,128)(2,1)} %proj_own_hbm.3) | copy-start | bytes 6291460
  82.3 6.4 %copy-start.5 = (s32[3]{0:T(128)S(1)}, s32[3]{0:T(128)}, u32[]{:S(2)}) copy-start(s32[3]{0:T(128)} %pad_add_fusion.place_ref) | copy-start | bytes 40
  82.3 6.4 %copy-start.8 = (s32[1,8,128]{2,1,0:T(8,128)S(1)}, s32[1,8,128]{2,1,0:T(8,128)}, u32[]{:S(2)}) copy-start(s32[1,8,128]{2,1,0:T(8,128)} %param.17) | copy-start | bytes 12292
  82.3 6.4 %copy-start.9 = (bf16[768,128]{1,0:T(8,128)(2,1)S(1)}, bf16[768,128]{1,0:T(8,128)(2,1)}, u32[]{:S(2)}) copy-start(bf16[768,128]{1,0:T(8,128)(2,1)} %get-tuple-element.37.refs_0_) | copy-start | bytes 589828
  87.4 0.8 copy-start.3
  88.2 49.5 %copy-start.2 = (bf16[512,512]{1,0:T(8,128)(2,1)}, bf16[512,512]{1,0:T(8,128)(2,1)S(1)}, u32[]{:S(2)}) copy-start(bf16[512,512]{1,0:T(8,128)(2,1)S(1)} %get-tuple-element.33.own_ref) | copy-start | bytes 1572868
  88.2 39.3 %collective-permute-start.14 = (bf16[512,2048]{1,0:T(8,128)(2,1)S(1)}, bf16[512,2048]{1,0:T(8,128)(2,1)S(1)}, u32[]{:S(2)}, u32[]{:S(2)}) collective-permute-start(bf16[512,2048]{1,0:T(8,128)(2,1)S(1)} %copy-done.10), channel_id=1, source_target_pairs={{0,4},{4,8},{8,12},{12,0},{16,28},{20,16},{24,20},{28,24},{1,5},{5... | collective-permute-start | bytes 6291464 | tf_op jit(solution)/shard_map/ppermute | solution.py:449
  127.5 10.1 %copy-start.12 = (bf16[512,2048]{1,0:T(8,128)(2,1)}, bf16[512,2048]{1,0:T(8,128)(2,1)S(1)}, u32[]{:S(2)}) copy-start(bf16[512,2048]{1,0:T(8,128)(2,1)S(1)} %collective-permute-done.14.proj_near_hbm) | copy-start | bytes 6291460
  127.5 10.1 %collective-permute-start.15 = (bf16[512,2048]{1,0:T(8,128)(2,1)S(1)}, bf16[512,2048]{1,0:T(8,128)(2,1)}, u32[]{:S(2)}, u32[]{:S(2)}) collective-permute-start(bf16[512,2048]{1,0:T(8,128)(2,1)S(1)} %collective-permute-done.14.proj_near_hbm), channel_id=1, source_target_pairs={{0,16},{16,0},{1,17},{17,1},{2,18},{18,2},{3,19},{19,3},{4,20},{20... | collective-permute-start | bytes 6291464 | tf_op jit(solution)/shard_map/ppermute | solution.py:469
  127.6 6.3 %collective-permute-start.11 = (bf16[256,128]{1,0:T(8,128)(2,1)S(1)}, bf16[256,128]{1,0:T(8,128)(2,1)S(1)}, u32[]{:S(2)}, u32[]{:S(2)}) collective-permute-start(bf16[256,128]{1,0:T(8,128)(2,1)S(1)} %get-tuple-element.42), channel_id=1, source_target_pairs={{0,12},{4,0},{8,4},{12,8},{1,13},{5,1},{9,5},{13,9},{2,14},{6,2},{... | collective-permute-start | bytes 196616 | tf_op jit(solution)/shard_map/ppermute | solution.py:436
  130.6 6.4 %collective-permute-start.12 = (bf16[256,128]{1,0:T(8,128)(2,1)S(1)}, bf16[256,128]{1,0:T(8,128)(2,1)S(1)}, u32[]{:S(2)}, u32[]{:S(2)}) collective-permute-start(bf16[256,128]{1,0:T(8,128)(2,1)S(1)} %get-tuple-element.43), channel_id=1, source_target_pairs={{0,8},{4,12},{8,0},{12,4},{1,9},{5,13},{9,1},{13,5},{2,10},{6,14},... | collective-permute-start | bytes 196616 | tf_op jit(solution)/shard_map/ppermute | solution.py:436
  131.2 6.5 %collective-permute-start.13 = (bf16[256,128]{1,0:T(8,128)(2,1)S(1)}, bf16[256,128]{1,0:T(8,128)(2,1)S(1)}, u32[]{:S(2)}, u32[]{:S(2)}) collective-permute-start(bf16[256,128]{1,0:T(8,128)(2,1)S(1)} %get-tuple-element.44), channel_id=1, source_target_pairs={{0,4},{4,8},{8,12},{12,0},{1,5},{5,9},{9,13},{13,1},{2,6},{6,10},{... | collective-permute-start | bytes 196616 | tf_op jit(solution)/shard_map/ppermute | solution.py:436
  145.4 0.8 copy-start.4
  146.2 10.4 %collective-permute-start.17 = (bf16[128,2048]{1,0:T(8,128)(2,1)S(1)}, bf16[128,2048]{1,0:T(8,128)(2,1)S(1)}, u32[]{:S(2)}, u32[]{:S(2)}) collective-permute-start(bf16[128,2048]{1,0:T(8,128)(2,1)S(1)} %get-tuple-element.51), channel_id=1, source_target_pairs={{0,1},{1,2},{2,3},{3,0},{16,19},{17,16},{18,17},{19,18},{4,5},{5,6... | collective-permute-start | bytes 1572872 | tf_op jit(solution)/shard_map/reduce_tokens/ppermute | solution.py:497
  157.0 14.3 %collective-permute-start.19 = (bf16[128,2048]{1,0:T(8,128)(2,1)S(1)}, bf16[128,2048]{1,0:T(8,128)(2,1)S(1)}, u32[]{:S(2)}, u32[]{:S(2)}) collective-permute-start(bf16[128,2048]{1,0:T(8,128)(2,1)S(1)} %get-tuple-element.54), channel_id=1, source_target_pairs={{0,3},{1,0},{2,1},{3,2},{4,7},{5,4},{6,5},{7,6},{8,11},{9,8},{10,9... | collective-permute-start | bytes 1572872 | tf_op jit(solution)/shard_map/reduce_tokens/ppermute | solution.py:504
  159.1 14.6 %collective-permute-start.18 = (bf16[128,2048]{1,0:T(8,128)(2,1)S(1)}, bf16[128,2048]{1,0:T(8,128)(2,1)S(1)}, u32[]{:S(2)}, u32[]{:S(2)}) collective-permute-start(bf16[128,2048]{1,0:T(8,128)(2,1)S(1)} %get-tuple-element.53), channel_id=1, source_target_pairs={{0,1},{1,2},{2,3},{3,0},{4,5},{5,6},{6,7},{7,4},{8,9},{9,10},{10,1... | collective-permute-start | bytes 1572872 | tf_op jit(solution)/shard_map/reduce_tokens/ppermute | solution.py:503
Sparse Core Ops, SparseCore 0:
  18.6 38.3 all-gather.4
  74.0 40.6 all-gather.6
